TPU v7x, 512 devices: a whole 4x8x8 slice. The times are simulated.
512 devices in a mesh: row: 32 (over y_hi, z), col: 16 (over x, y_lo, core).
Axes of the slice: x: 4, y: 8 (y_hi: 4, y_lo: 2; y = y_hi * 2 + y_lo), z: 8, core: 2. Of those that a mesh axis runs over, the one named last changes fastest.
Arguments:
- anc_inverse: bfloat16 [1, 32, 256, 2, 16, 256], P(None, 'row', None, None, 'col'), may hold values from -6 to 6
- factor_one: bfloat16 [1, 32, 256, 2, 16, 256], P(None, 'row', None, None, 'col'), may hold values from -0.0625 to 0.0625
- factor_two: bfloat16 [1, 32, 256, 1, 16, 256], P(None, 'row', None, None, 'col'), may hold values from -0.0625 to 0.0625
- parent_block: bfloat16 [1, 16, 256, 256], P(None, 'col'), may hold values from -0.375 to 0.375
- diag_one: float32 [2, 16, 256, 256], P(None, 'col'), may hold values from -6 to 6
- diag_two: float32 [1, 16, 256, 256], P(None, 'col'), may hold values from -6 to 6
- pattern_one: int32 [1, 32, 2, 16], P(None, 'row', None, 'col'), may hold values from 0 to 1
- pattern_two: int32 [1, 32, 1, 16], P(None, 'row', None, 'col'), may hold values from 0 to 1, as said below
- parent: int32 [1, 16], P(None, 'col'), may hold values from 0 to 31, as said below
Outputs:
- inv_one: bfloat16 [1, 32, 256, 2, 16, 256], P(None, 'row', None, None, 'col')
- diag_inv_one: float32 [2, 16, 256, 256], P(None, 'col')
- inv_two: bfloat16 [1, 32, 256, 1, 16, 256], P(None, 'row', None, None, 'col')
- parent_inv: bfloat16 [1, 16, 256, 256], P(None, 'col')
- diag_inv_two: float32 [1, 16, 256, 256], P(None, 'col')
Inputs may be any that keep to these rules, and one draw needn't show every extreme that they name: pattern_two[J, K] is zero wherever pattern_one[J, P(K)] is zero. parent[k, c] is a level-one supernode whose index leaves remainder c when divided by 16.
All inputs are finite; a program needn't handle non-finite values.
Results may differ from a plain program's by a relative error of at most 0.007.
Values may be sent and summed in bfloat16 or wider, within the bound.
A program may use at most 64 MiB of HBM per device.

v0:
```python
import jax
import jax.numpy as jnp
from jax import lax
from jax.sharding import PartitionSpec as P


def rows_step(whole_anc, anc_rows, block):

    def add_rows(total, piece, start):
        count = piece.shape[1]
        left = whole_anc.reshape(anc_rows * block, anc_rows * count * block)
        right = piece.reshape(anc_rows * count * block, piece.shape[3] * block)
        return jnp.dot(left, right, preferred_element_type=jnp.float32)

    return add_rows


def body(
    anc_inverse,
    factor_one,
    factor_two,
    parent_block,
    diag_one,
    diag_two,
    pattern_one,
    pattern_two,
    parent,
):
    anc_rows = anc_inverse.shape[0]
    block = anc_inverse.shape[2]
    first_count = factor_one.shape[3]
    second_count = factor_two.shape[3]
    grid_rows = lax.axis_size("row")
    grid_cols = lax.axis_size("col")
    first_factor = factor_one * pattern_one.astype(jnp.bfloat16)[:, :, None, :, :, None]
    second_factor = factor_two * pattern_two.astype(jnp.bfloat16)[:, :, None, :, :, None]
    first_empty = jnp.zeros((anc_rows * block, first_count * block), jnp.float32)
    second_empty = jnp.zeros((anc_rows * block, second_count * block), jnp.float32)
    whole_anc = lax.all_gather(anc_inverse, "col", axis=4, tiled=True).reshape(
        anc_rows * block, anc_rows, grid_rows, block
    )
    add_rows = rows_step(whole_anc, anc_rows, block)
    first_total = add_rows(
        first_empty, lax.all_gather(first_factor, "row", axis=1, tiled=True), jnp.int32(0)
    )
    first_shape = (anc_rows, block, first_count, block)
    second_shape = (anc_rows, block, second_count, block)
    first_keep = pattern_one.astype(jnp.float32)
    second_keep = pattern_two.astype(jnp.float32)
    first_inv = (-first_total.reshape(first_shape) * first_keep).astype(jnp.bfloat16)
    first_cols = first_factor.reshape(first_shape)
    second_cols = second_factor.reshape(second_shape)
    diag_part = jnp.einsum(
        "ixky,ixkz->kyz", first_cols, first_inv, preferred_element_type=jnp.float32
    )
    local_parent = parent.reshape(second_count) // grid_cols
    parent_cols = jnp.take(first_inv, local_parent, axis=2)
    cross_part = jnp.einsum(
        "ixky,ixkz->kyz", parent_cols, second_cols, preferred_element_type=jnp.float32
    )
    diag_sum, cross_sum = lax.psum((diag_part, cross_part), "row")
    first_diag = diag_one.reshape(first_count, block, block) - diag_sum
    parent_diag = jnp.take(first_diag.astype(jnp.bfloat16), local_parent, axis=0)
    coupling = parent_block.reshape(second_count, block, block)
    parent_inv = (
        -(
            jnp.einsum("kyx,kxz->kyz", parent_diag, coupling, preferred_element_type=jnp.float32)
            + cross_sum
        )
    ).astype(jnp.bfloat16)
    second_total = add_rows(
        second_empty, lax.all_gather(second_factor, "row", axis=1, tiled=True), jnp.int32(0)
    )
    side = jnp.einsum("ixky,kyz->ixkz", parent_cols, coupling, preferred_element_type=jnp.float32)
    second_inv = (-(second_total.reshape(second_shape) + side) * second_keep).astype(jnp.bfloat16)
    child_part = jnp.einsum(
        "ixky,ixkz->kyz", second_cols, second_inv, preferred_element_type=jnp.float32
    )
    child_sum = lax.psum(child_part.astype(jnp.bfloat16), "row").astype(jnp.float32)
    parent_terms = jnp.einsum(
        "kxy,kxz->kyz", coupling, parent_inv, preferred_element_type=jnp.float32
    )
    second_diag = diag_two.reshape(second_count, block, block) - (child_sum + parent_terms)
    return (
        first_inv.reshape(factor_one.shape),
        first_diag.reshape(diag_one.shape),
        second_inv.reshape(factor_two.shape),
        parent_inv.reshape(parent_block.shape),
        second_diag.reshape(diag_two.shape),
    )


def solution(mesh):
    placed = (
        P(None, "row", None, None, "col", None),
        P(None, "row", None, None, "col", None),
        P(None, "row", None, None, "col", None),
        P(None, "col", None, None),
        P(None, "col", None, None),
        P(None, "col", None, None),
        P(None, "row", None, "col"),
        P(None, "row", None, "col"),
        P(None, "col"),
    )
    return jax.shard_map(
        body,
        mesh=mesh,
        in_specs=placed,
        out_specs=(
            P(None, "row", None, None, "col", None),
            P(None, "col", None, None),
            P(None, "row", None, None, "col", None),
            P(None, "col", None, None),
            P(None, "col", None, None),
        ),
        check_vma=False,
    )
```

profile of v0, /device:TPU:1, one launch (start us, length us, event | category | flops | bytes accessed | tf_op | source)
XLA Modules:
  0.0 904.1 jit_solution(8874706373367763510)
XLA Ops:
  7.2 0.0 copy-start
  7.2 0.0 all-gather.4.cloned.1.call-start
  7.2 0.7 convert_bitcast_fusion
  8.0 1.7 copy_multiply_fusion
  9.7 0.0 all-gather.4.cloned.1.call-update
  9.7 0.0 all-gather.6.cloned.1.call-start
  9.8 1.8 copy.41
  11.6 0.0 all-gather.6.cloned.1.call-update
  11.6 0.0 all-gather.8.cloned.1.call-start
  12.3 1.6 bitcast_multiply_fusion
  13.9 0.0 all-gather.8.cloned.1.call-update
  13.9 0.0 all-reduce.6.cloned.1.call-start
  14.6 0.6 dynamic-slice.9
  15.2 140.7 %all-gather.4.cloned.1.call-done = bf16[1,32,256,2,1,256]{5,2,4,3,0,1:T(8,128)(2,1)} async-done(((bf16[1,1,256,2,1,256]{5,2,4,3,0,1:T(8,128)(2,1)}), bf16[1,32,256,2,1,256]{5,2,4,3,0,1:T(8,128)(2,1)}) %all-gather.4.cloned.1.call-update) | async-done | bytes 8388624 | tf_op jit(solution)/shard_map/all_gather | solution.py:44
  155.9 14.6 %copy.40 = bf16[1,32,256,2,1,256]{2,1,5,3,4,0:T(8,128)(2,1)} copy(bf16[1,32,256,2,1,256]{5,2,4,3,0,1:T(8,128)(2,1)} %all-gather.4.cloned.1.call-done) | data formatting | bytes 16777216 | tf_op jit(solution)/shard_map/all_gather | solution.py:44
  170.5 16.5 %copy.53 = bf16[64,8,32,256]{3,1,2,0:T(8,128)(2,1)} copy(bf16[64,8,32,256]{3,2,1,0:T(8,128)(2,1)} %bitcast.112) | data formatting | bytes 16777216
  187.0 11.4 %all-gather.6.cloned.1.call-done = bf16[1,1,256,2,16,256]{2,5,4,3,1,0:T(8,128)(2,1)} async-done(((bf16[1,1,256,2,1,256]{2,5,4,3,1,0:T(8,128)(2,1)}), bf16[1,1,256,2,16,256]{2,5,4,3,1,0:T(8,128)(2,1)}) %all-gather.6.cloned.1.call-update) | async-done | bytes 4194320 | tf_op jit(solution)/shard_map/all_gather | solution.py:39
  198.4 0.0 copy-start.2
  198.4 0.0 copy-start.1
  198.4 7.2 convolution_negate_fusion
  205.5 0.2 copy.43
  205.7 0.0 copy-done.2
  205.7 1.5 convolution_bitcast_fusion.1
  207.3 0.0 copy-done.1
  207.3 1.1 fusion.11
  208.4 0.0 all-reduce.6.cloned.1.call-update
  208.4 0.0 all-reduce.4.cloned.1.call-start
  208.4 94.0 %all-gather.8.cloned.1.call-done = bf16[1,32,256,1,1,256]{5,2,4,3,0,1:T(8,128)(2,1)} async-done(((bf16[1,1,256,1,1,256]{5,2,4,3,0,1:T(8,128)(2,1)}), bf16[1,32,256,1,1,256]{5,2,4,3,0,1:T(8,128)(2,1)}) %all-gather.8.cloned.1.call-update) | async-done | bytes 4194320 | tf_op jit(solution)/shard_map/all_gather | solution.py:72
  302.5 0.0 copy-start.4
  302.5 4.8 convolution_bitcast_fusion.4
  307.3 0.0 copy-start.6
  307.3 0.2 copy.42
  307.5 0.0 copy-done
  307.5 0.9 fusion.9
  308.4 0.8 copy.49
  309.2 0.9 fusion.10
  310.1 0.9 multiply_convert_fusion.1
  311.0 0.0 all-reduce.4.cloned.1.call-update
  311.0 289.7 %all-reduce.6.cloned.1.call-done = (f32[2,256,256]{2,1,0:T(8,128)}, f32[1,256,256]{2,1,0:T(8,128)}) async-done(((f32[2,256,256]{2,1,0:T(8,128)}, f32[1,256,256]{2,1,0:T(8,128)}), (f32[2,256,256]{2,1,0:T(8,128)}, f32[1,256,256]{2,1,0:T(8,128)})) %all-reduce.6.cloned.1.call-update) | async-done | bytes 786448 | tf_op jit(solution)/shard_map/psum | solution.py:61
  600.8 0.0 copy-done.4
  600.8 1.1 bitcast_subtract_fusion
  601.9 0.0 copy-start.3
  601.9 1.3 fusion.8
  603.2 0.0 copy-start.5
  603.2 292.4 %all-reduce.4.cloned.1.call-done = bf16[1,256,256]{2,1,0:T(8,128)(2,1)} async-done(((bf16[1,256,256]{2,1,0:T(8,128)(2,1)}), bf16[1,256,256]{2,1,0:T(8,128)(2,1)}) %all-reduce.4.cloned.1.call-update) | async-done | bytes 131088 | tf_op jit(solution)/shard_map/psum | solution.py:79
  895.7 0.0 copy-done.6
  895.7 1.8 fusion.7
  897.5 0.0 copy-done.3
  897.5 0.0 copy-done.5
Async XLA Ops:
  7.2 300.4 %copy-start = (bf16[1,1,256,256]{3,2,1,0:T(8,128)(2,1)S(1)}, bf16[1,1,256,256]{3,2,1,0:T(8,128)(2,1)}, u32[]{:S(2)}) copy-start(bf16[1,1,256,256]{3,2,1,0:T(8,128)(2,1)} %param.12) | copy-start | bytes 393220
  7.2 148.7 %all-gather.4.cloned.1.call-start = ((), (), s32[]{:S(2)}) async-start(), calls=%async_computation | async-start | bytes 8650752 | tf_op jit(solution)/shard_map/all_gather | solution.py:44
  9.7 188.6 %all-gather.6.cloned.1.call-start = ((), (), s32[]{:S(2)}) async-start(), calls=%async_computation.1 | async-start | bytes 4456448 | tf_op jit(solution)/shard_map/all_gather | solution.py:39
  11.6 290.9 %all-gather.8.cloned.1.call-start = ((), (), s32[]{:S(2)}) async-start(), calls=%async_computation.2 | async-start | bytes 4325376 | tf_op jit(solution)/shard_map/all_gather | solution.py:72
  13.9 586.8 %all-reduce.6.cloned.1.call-start = ((), (), s32[]{:S(2)}) async-start(), calls=%async_computation.4 | async-start | bytes 1572864 | tf_op jit(solution)/shard_map/psum | solution.py:61
  198.4 7.4 copy-start.2
  198.4 8.9 copy-start.1
  208.4 687.3 %all-reduce.4.cloned.1.call-start = ((), (), s32[]{:S(2)}) async-start(), calls=%async_computation.3 | async-start | bytes 262144 | tf_op jit(solution)/shard_map/psum | solution.py:79
  302.5 298.3 %copy-start.4 = (f32[2,1,256,256]{3,2,1,0:T(8,128)S(1)}, f32[2,1,256,256]{3,2,1,0:T(8,128)}, u32[]{:S(2)}) copy-start(f32[2,1,256,256]{3,2,1,0:T(8,128)} %param.13) | copy-start | bytes 1572868
  307.3 588.4 %copy-start.6 = (f32[1,1,256,256]{3,2,1,0:T(8,128)S(1)}, f32[1,1,256,256]{3,2,1,0:T(8,128)}, u32[]{:S(2)}) copy-start(f32[1,1,256,256]{3,2,1,0:T(8,128)} %param.14) | copy-start | bytes 786436
  601.9 295.7 %copy-start.3 = (f32[2,256,256]{2,1,0:T(8,128)}, f32[2,256,256]{2,1,0:T(8,128)S(1)}, u32[]{:S(2)}) copy-start(f32[2,256,256]{2,1,0:T(8,128)S(1)} %bitcast_subtract_fusion) | copy-start | bytes 1572868
  603.2 294.3 %copy-start.5 = (bf16[1,256,256]{2,1,0:T(8,128)(2,1)}, bf16[1,256,256]{2,1,0:T(8,128)(2,1)S(1)}, u32[]{:S(2)}) copy-start(bf16[1,256,256]{2,1,0:T(8,128)(2,1)S(1)} %fusion.8) | copy-start | bytes 393220
Sparse Core Ops, SparseCore 0:
  11.8 144.0 all-gather.3
  158.5 39.7 all-gather.5
  202.1 100.3 all-gather.7
  305.9 294.8 all-reduce.5
  604.3 291.2 all-reduce.3
where the time goes:
time: 918 us; the launch traced here: 904 us
  waiting for transfers between devices  828 us (90%)
  local copies, waits for them, and re-layouts  34.7 us (4%)
  matrix products  19.5 us (2%)
  between operations  15.2 us (2%)
    psum x1, waiting for transfers between devices, body(): lax.psum(child_part.astype(jnp.bfloat16), 'row').astype(jnp.float32)  292 us
    psum x1, waiting for transfers between devices, body(): diag_sum, cross_sum = lax.psum((diag_part, cross_part), 'row')  290 us
    all_gather x1, waiting for transfers between devices, body(): lax.all_gather(first_factor, 'row', axis=1, tiled=True)  141 us
    all_gather x1, waiting for transfers between devices, body(): lax.all_gather(second_factor, 'row', axis=1, tiled=True)  94 us
    unnamed x17, local copies, waits for them, and re-layouts  19.1 us
  transfers between devices with their start and end apart: 5, of which 5 were waited for; matrix products, arithmetic and copies ran while one was open for 6% of the time, Pallas kernels for 0%

commit v1 on v0

v1 whole, which is shorter than its diff:
```python
import functools

import jax
import jax.numpy as jnp
from jax import lax
from jax.experimental import pallas as pl
from jax.experimental.pallas import tpu as pltpu
from jax.sharding import PartitionSpec as P

MESH = pl.DeviceIdType.MESH
B = 256
NY, NZ, NX = 4, 8, 4
ROWS = NY * NZ
WIDE = 3 * B
SLICE = 4 * B // ROWS


def mm(a, b):
    return jnp.dot(a, b, preferred_element_type=jnp.float32)


def mm_t(a, b):
    return lax.dot_general(a, b, (((0,), (0,)), ((), ())), preferred_element_type=jnp.float32)


def kernel(
    p1_ref, p2_ref, par_ref, a_ref, f_ref, pb_ref, d1_ref, d2_ref,
    inv1_ref, diag1_ref, inv2_ref, pinv_ref, diag2_ref,
    f_all, a_all, acc, c_send, c_recv, parts, r_recv, r_out,
    fs, fr, a1s, a1r, xs, xr, ys, yr, cs, cr, rs, rr, s1, r1, s2, r2, own_sem,
):
    row, col = lax.axis_index("row"), lax.axis_index("col")
    y, z = row // NZ, row % NZ
    x, yl, core = col // 4, (col // 2) % 2, col % 2

    def remote(src, dst, ss, rs_, to_row, to_col):
        return pltpu.make_async_remote_copy(
            src_ref=src, dst_ref=dst, send_sem=ss, recv_sem=rs_,
            device_id=(to_row, to_col), device_id_type=MESH,
        )

    def row_at(d):
        return lax.rem(row + d, ROWS)

    def col_of(x_, yl_, core_):
        return x_ * 4 + yl_ * 2 + core_

    y_mate = col_of(x, 1 - yl, core)
    c_mate = col_of(x, yl, 1 - core)

    barrier = pltpu.get_barrier_semaphore()

    def greet(d, carry):
        pl.semaphore_signal(barrier, inc=1, device_id=(row_at(d), col), device_id_type=MESH)
        return carry

    lax.fori_loop(1, ROWS, greet, 0)
    for dx in range(1, NX):
        pl.semaphore_signal(
            barrier, inc=1, device_id=(row, col_of(lax.rem(x + dx, NX), yl, core)), device_id_type=MESH
        )
    pl.semaphore_signal(barrier, inc=1, device_id=(row, y_mate), device_id_type=MESH)
    pl.semaphore_signal(barrier, inc=1, device_id=(row, c_mate), device_id_type=MESH)
    pl.semaphore_wait(barrier, ROWS - 1 + NX - 1 + 2)

    up = y * NZ + lax.rem(z + 1, NZ)
    down = y * NZ + lax.rem(z + NZ - 1, NZ)
    half = B // 2

    def f_copies(step):
        up_slot = lax.rem(z + NZ - step, NZ)
        down_slot = lax.rem(z + step, NZ)
        if step == 0:
            u_src, d_src = f_ref, f_ref
        elif step < 3:
            u_src, d_src = f_all.at[up_slot], f_all.at[down_slot]
        if step < 3:
            u_dst, d_dst = f_all.at[up_slot], f_all.at[down_slot]
        else:
            u_src = u_dst = f_all.at[up_slot, pl.ds(0, half)]
            d_src = d_dst = f_all.at[down_slot, pl.ds(half, half)]
        return (
            remote(u_src, u_dst, fs.at[0, step], fr.at[0, step], up, col),
            remote(d_src, d_dst, fs.at[1, step], fr.at[1, step], down, col),
        )

    def f_start(step):
        for copy in f_copies(step):
            copy.start()

    def f_arrived(step):
        for copy in f_copies(step):
            copy.wait_recv()

    slot = lax.rem(col, NZ)
    holder = lax.rem(y, 2) == x // 2

    def a1_copy(h):
        return remote(
            a_ref.at[h], a_all.at[slot, y], a1s.at[h], a1r.at[y], (2 * h + x // 2) * NZ + z, col
        )

    def own_copy(h):
        return pltpu.make_async_copy(a_ref.at[h], a_all.at[slot, y], own_sem)

    f_start(0)
    for h in range(2):
        target = 2 * h + x // 2

        @pl.when(target != y)
        def _():
            a1_copy(h).start()

        @pl.when(target == y)
        def _():
            own_copy(h).start()

    def slot_of(s, yl_, core_):
        return s * 4 + yl_ * 2 + core_

    def x_copy(s, dx):
        k = slot_of(s, yl, core)
        return remote(
            a_all.at[k], a_all.at[k], xs.at[dx - 1], xr.at[s], row, col_of(lax.rem(x + dx, NX), yl, core)
        )

    def y_copy(s):
        k = slot_of(s, yl, core)
        return remote(a_all.at[k], a_all.at[k], ys.at[s], yr.at[s], row, y_mate)

    def y_here(s):
        k = slot_of(s, 1 - yl, core)
        return remote(a_all.at[k], a_all.at[k], ys.at[s], yr.at[s], row, y_mate)

    def c_copy(s, yl_):
        k = slot_of(s, yl_, core)
        return remote(a_all.at[k], a_all.at[k], cs.at[s, yl_], cr.at[s, yl_], row, c_mate)

    def c_here(s, yl_):
        k = slot_of(s, yl_, 1 - core)
        return remote(a_all.at[k], a_all.at[k], cs.at[s, yl_], cr.at[s, yl_], row, c_mate)

    f_all[z] = f_ref[...]
    f_arrived(0)
    f_start(1)

    @pl.when(holder)
    def _():
        own_copy(0).wait()
        for k in range(1, NY):
            other = lax.rem(y + k, NY)
            remote(
                a_ref.at[0], a_all.at[slot, other], a1s.at[0], a1r.at[other], row_at(1), col
            ).wait_recv()
        s = lax.rem(x, 2)
        for dx in (2, 1, 3):
            x_copy(s, dx).start()

    f_arrived(1)
    f_start(2)
    for s in range(2):
        source = 2 * lax.rem(y, 2) + s

        @pl.when(source != x)
        def _():
            x_copy(s, 1).wait_recv()

        y_copy(s).start()
        c_copy(s, yl).start()
    f_arrived(2)
    f_start(3)
    for s in range(2):
        y_here(s).wait_recv()
        c_copy(s, 1 - yl).start()
    f_arrived(3)
    for s in range(2):
        for yl_ in range(2):
            c_here(s, yl_).wait_recv()

    def partial_product(y_):
        acc[...] = mm(a_all[0, y_], f_all[0])

        def step(k, carry):
            acc[...] += mm(a_all[k, y_], f_all[k])
            return carry

        lax.fori_loop(1, NZ, step, 0)

    def c_part(k):
        return remote(
            c_send.at[k - 1], c_recv.at[k - 1], rs.at[k - 1], rr.at[k - 1], lax.rem(y + k, NY) * NZ + z, col
        )

    for k in (2, 1, 3):
        partial_product(lax.rem(y + k, NY))
        c_send[k - 1] = acc[...].astype(jnp.bfloat16)
        c_part(k).start()
    partial_product(y)
    for k in (1, 3, 2):
        c_part(k).wait_recv()
    total = acc[...]
    for k in (1, 2, 3):
        total += c_recv[k - 1].astype(jnp.float32)

    m0 = p1_ref[0].astype(jnp.float32)
    m1 = p1_ref[1].astype(jnp.float32)
    m2 = p2_ref[0].astype(jnp.float32)
    second = par_ref[0] >= 16
    inv_a = (-total[:, :B] * m0).astype(jnp.bfloat16)
    inv_b = (-total[:, B : 2 * B] * m1).astype(jnp.bfloat16)
    parent_cols = jnp.where(second, inv_b, inv_a)
    pb = pb_ref[...]
    side = mm(parent_cols, pb)
    inv_c = (-(total[:, 2 * B :] + side) * m2).astype(jnp.bfloat16)
    inv1_ref[0] = inv_a
    inv1_ref[1] = inv_b
    inv2_ref[...] = inv_c
    per = B // SLICE

    def put(i, value):
        parts[pl.ds(i * per, per)] = value.astype(jnp.bfloat16).reshape(per, SLICE, B)

    put(0, mm_t(f_ref[:, :B], inv_a))
    put(1, mm_t(f_ref[:, B : 2 * B], inv_b))
    put(2, mm_t(parent_cols, f_ref[:, 2 * B :]))
    put(3, mm_t(f_ref[:, 2 * B :], inv_c))

    def first(d):
        return remote(parts.at[row_at(d)], r_recv.at[d], s1.at[d], r1.at[d], row_at(d), col)

    def second_copy(d):
        return remote(r_out.at[row], r_out.at[row], s2.at[d], r2.at[d], row_at(d), col)

    def loop(body):
        def step(d, carry):
            body(d)
            return carry

        lax.fori_loop(1, ROWS, step, 0)

    loop(lambda d: first(d).start())
    r_recv[0] = parts[row]
    loop(lambda d: first(d).wait_recv())
    r_out[row] = jnp.sum(r_recv[...].astype(jnp.float32), axis=0).astype(jnp.bfloat16)
    loop(lambda d: second_copy(d).start())
    loop(lambda d: second_copy(d).wait_recv())

    def block(i):
        return r_out[pl.ds(i * per, per)].reshape(B, B).astype(jnp.float32)

    diag_a = d1_ref[0] - block(0)
    diag_b = d1_ref[1] - block(1)
    diag1_ref[0] = diag_a
    diag1_ref[1] = diag_b
    parent_diag = jnp.where(second, diag_b, diag_a).astype(jnp.bfloat16)
    pinv = (-(mm(parent_diag, pb) + block(2))).astype(jnp.bfloat16)
    pinv_ref[...] = pinv
    diag2_ref[...] = d2_ref[...] - (block(3) + mm_t(pb, pinv))

    for step in range(4):
        for copy in f_copies(step):
            copy.wait_send()
    for h in range(2):

        @pl.when(2 * h + x // 2 != y)
        def _():
            a1_copy(h).wait_send()

    @pl.when(holder)
    def _():
        for dx in range(1, NX):
            x_copy(0, dx).wait_send()

    for s in range(2):
        y_copy(s).wait_send()
        for yl_ in range(2):
            c_copy(s, yl_).wait_send()
    for k in range(1, NY):
        c_part(k).wait_send()
    loop(lambda d: first(d).wait_send())
    loop(lambda d: second_copy(d).wait_send())


def body(anc, one, two, pb, d1, d2, p1, p2, par):
    a = anc.reshape(B, 2, B).transpose(1, 0, 2)
    f1 = one.reshape(B, 2, B) * p1.reshape(1, 2, 1).astype(jnp.bfloat16)
    f2 = two.reshape(B, 1, B) * p2.reshape(1, 1, 1).astype(jnp.bfloat16)
    f = jnp.concatenate([f1, f2], axis=1).reshape(B, WIDE)
    vmem = pl.BlockSpec(memory_space=pltpu.VMEM)
    smem = pl.BlockSpec(memory_space=pltpu.SMEM)
    dma = pltpu.SemaphoreType.DMA
    bf, f32 = jnp.bfloat16, jnp.float32
    inv1, diag1, inv2, pinv, diag2 = pl.pallas_call(
        kernel,
        out_shape=(
            jax.ShapeDtypeStruct((2, B, B), bf),
            jax.ShapeDtypeStruct((2, B, B), f32),
            jax.ShapeDtypeStruct((B, B), bf),
            jax.ShapeDtypeStruct((B, B), bf),
            jax.ShapeDtypeStruct((B, B), f32),
        ),
        in_specs=[smem] * 3 + [vmem] * 5,
        out_specs=(vmem,) * 5,
        scratch_shapes=[
            pltpu.VMEM((NZ, B, WIDE), bf),
            pltpu.VMEM((NZ, NY, B, B), bf),
            pltpu.VMEM((B, WIDE), f32),
            pltpu.VMEM((3, B, WIDE), bf),
            pltpu.VMEM((3, B, WIDE), bf),
            pltpu.VMEM((ROWS, SLICE, B), bf),
            pltpu.VMEM((ROWS, SLICE, B), bf),
            pltpu.VMEM((ROWS, SLICE, B), bf),
            dma((2, 4)), dma((2, 4)),
            dma((2,)), dma((NY,)),
            dma((3,)), dma((2,)),
            dma((2,)), dma((2,)),
            dma((2, 2)), dma((2, 2)),
            dma((3,)), dma((3,)),
            dma((ROWS,)), dma((ROWS,)),
            dma((ROWS,)), dma((ROWS,)),
            dma(()),
        ],
        compiler_params=pltpu.CompilerParams(
            collective_id=0, has_side_effects=True, vmem_limit_bytes=40 * 1024 * 1024
        ),
    )(
        p1.reshape(2), p2.reshape(1), par.reshape(1), a, f,
        pb.reshape(B, B), d1.reshape(2, B, B), d2.reshape(B, B),
    )
    return (
        inv1.transpose(1, 0, 2).reshape(one.shape),
        diag1.reshape(d1.shape),
        inv2.reshape(two.shape),
        pinv.reshape(pb.shape),
        diag2.reshape(d2.shape),
    )


def solution(mesh):
    placed = (
        P(None, "row", None, None, "col", None),
        P(None, "row", None, None, "col", None),
        P(None, "row", None, None, "col", None),
        P(None, "col", None, None),
        P(None, "col", None, None),
        P(None, "col", None, None),
        P(None, "row", None, "col"),
        P(None, "row", None, "col"),
        P(None, "col"),
    )
    return jax.shard_map(
        body,
        mesh=mesh,
        in_specs=placed,
        out_specs=(
            P(None, "row", None, None, "col", None),
            P(None, "col", None, None),
            P(None, "row", None, None, "col", None),
            P(None, "col", None, None),
            P(None, "col", None, None),
        ),
        check_vma=False,
    )
```

time: 918 us -> 159 us (0.17)
  the two profiles are of different devices: /device:TPU:1 before, /device:TPU:2 now
where the time goes in v1:
time: 159 us
  Pallas kernels  149 us (94%)
  local copies, waits for them, and re-layouts  7.7 us (5%)
  between operations  2.04 us (1%)
    pallas_call x1, Pallas kernels, body(): pl.pallas_call(kernel, out_shape=(jax.ShapeDtypeStruct((2, B, B), bf), ja...  149 us
    unnamed x20, local copies, waits for them, and re-layouts  7.52 us

profile of v1, /device:TPU:2, one launch (start us, length us, event | category | flops | bytes accessed | tf_op | source)
XLA Modules:
  0.0 158.8 jit_solution(15778388584558642920)
XLA Ops:
  1.9 0.0 copy-start.3
  1.9 0.6 copy-done.3
  2.6 0.0 copy-start.4
  2.6 1.0 copy.20
  3.7 0.0 copy-done.4
  3.7 0.0 copy-start.5
  3.7 0.9 copy-done.5
  4.6 0.2 copy.19
  4.8 0.1 bitcast_multiply_fusion
  4.9 0.0 copy-start.2
  5.0 0.0 copy-start
  5.0 0.0 copy-start.1
  5.0 0.2 copy.21.f_ref
  5.2 0.6 copy-done.2
  5.8 0.2 copy-done
  6.0 0.1 copy-done.1
  6.1 148.9 %shard_map.128 = (bf16[2,256,256]{2,1,0:T(8,128)(2,1)S(1)}, f32[2,256,256]{2,1,0:T(8,128)S(1)}, bf16[256,256]{1,0:T(8,128)(2,1)S(1)}, bf16[256,256]{1,0:T(8,128)(2,1)S(1)}, f32[256,256]{1,0:T(8,128)S(1)}) custom-call(s32[2]{0:T(128)S(1)} %bitcast.38, s32[1]{0:T(128)} %bitcast.27.p2_ref, s32[1]{0:T(128)} %bitcast.28.par_ref, ...), custom_call_target="tpu_custom_call" | custom-call | tf_op jit(solution)/shard_map/pallas_call | solution.py:293
  155.0 1.0 copy.22
  156.0 0.8 copy.32
  156.8 0.7 copy.33
  157.4 0.7 copy.34
  158.1 0.7 copy.35
  (4 shorter events, 0.1 us)
Async XLA Ops:
  1.9 0.7 copy-start.3
  2.6 1.1 copy-start.4
  3.7 1.0 copy-start.5
  4.9 0.9 copy-start.2
  5.0 1.1 copy-start
  5.0 1.1 copy-start.1

commit v2 on v1

v2 whole, which is shorter than its diff:
```python
import functools

import jax
import jax.numpy as jnp
from jax import lax
from jax.experimental import pallas as pl
from jax.experimental.pallas import tpu as pltpu
from jax.sharding import PartitionSpec as P

MESH = pl.DeviceIdType.MESH
B = 256
NY, NZ, NX = 4, 8, 4
ROWS = NY * NZ
SLICE = 4 * B // ROWS


def mm(a, b):
    return jnp.dot(a, b, preferred_element_type=jnp.float32)


def mm_t(a, b):
    return lax.dot_general(a, b, (((0,), (0,)), ((), ())), preferred_element_type=jnp.float32)


def kernel(
    p1_ref, p2_ref, par_ref, a_ref, f1_ref, f2_ref, pb_ref, d1_ref, d2_ref,
    inv1_ref, diag1_ref, inv2_ref, pinv_ref, diag2_ref,
    f_all, a_all, acc, e_send, e_recv, p_send, p_recv, g_send, g_recv, parts, r_recv, r_out,
    fs, fr, a1s, a1r, os, orr, xs, xr, ys, yr, cs, cr, es, er, ps, pr, gs, gr, s1, r1, s2, r2, own_sem,
):
    row, col = lax.axis_index("row"), lax.axis_index("col")
    y, z = row // NZ, row % NZ
    x, yl, core = col // 4, (col // 2) % 2, col % 2

    def remote(src, dst, ss, rs_, to_row, to_col):
        return pltpu.make_async_remote_copy(
            src_ref=src, dst_ref=dst, send_sem=ss, recv_sem=rs_,
            device_id=(to_row, to_col), device_id_type=MESH,
        )

    def row_at(d):
        return lax.rem(row + d, ROWS)

    def col_of(x_, yl_, core_):
        return x_ * 4 + yl_ * 2 + core_

    y_mate = col_of(x, 1 - yl, core)
    c_mate = col_of(x, yl, 1 - core)
    across = col_of(x + 1 - 2 * lax.rem(x, 2), yl, core)
    outward = col_of(NX - 1 - x, yl, core)

    barrier = pltpu.get_barrier_semaphore()

    def greet(d, carry):
        pl.semaphore_signal(barrier, inc=1, device_id=(row_at(d), col), device_id_type=MESH)
        return carry

    lax.fori_loop(1, ROWS, greet, 0)
    for mate in (across, outward, y_mate, c_mate):
        pl.semaphore_signal(barrier, inc=1, device_id=(row, mate), device_id_type=MESH)
    m0 = p1_ref[0].astype(jnp.float32)
    m1 = p1_ref[1].astype(jnp.float32)
    m2 = p2_ref[0].astype(jnp.float32)
    f_all[0, z] = f1_ref[0] * m0.astype(jnp.bfloat16)
    f_all[1, z] = f1_ref[1] * m1.astype(jnp.bfloat16)
    f_all[2, z] = f2_ref[...] * m2.astype(jnp.bfloat16)
    pl.semaphore_wait(barrier, ROWS - 1 + 4)

    up = y * NZ + lax.rem(z + 1, NZ)
    down = y * NZ + lax.rem(z + NZ - 1, NZ)
    half = B // 2

    def f_copies(step, k):
        up_slot = lax.rem(z + NZ - step, NZ)
        down_slot = lax.rem(z + step, NZ)
        if step < 3:
            u, d = f_all.at[k, up_slot], f_all.at[k, down_slot]
        else:
            u = f_all.at[k, up_slot, pl.ds(0, half)]
            d = f_all.at[k, down_slot, pl.ds(half, half)]
        return (
            remote(u, u, fs.at[0, step, k], fr.at[0, step, k], up, col),
            remote(d, d, fs.at[1, step, k], fr.at[1, step, k], down, col),
        )

    def f_step(step):
        for k in range(3):
            if step > 0:
                for copy in f_copies(step - 1, k):
                    copy.wait_recv()
            if step < 4:
                for copy in f_copies(step, k):
                    copy.start()

    slot = lax.rem(col, NZ)
    hold = lax.rem(y + x // 2 + 1, 2)
    near = lax.rem(x + 1 + hold, 2)

    def a1_copy(h):
        return remote(
            a_ref.at[h], a_all.at[slot, y], a1s.at[h], a1r.at[y], (2 * h + x // 2) * NZ + z, col
        )

    def own_copy(h):
        return pltpu.make_async_copy(a_ref.at[h], a_all.at[slot, y], own_sem)

    for h in range(2):
        target = 2 * h + x // 2

        @pl.when(target != y)
        def _():
            a1_copy(h).start()

        @pl.when(target == y)
        def _():
            own_copy(h).start()

    f_step(0)

    def chunk(far, yl_, core_, k):
        s = 1 - near if far else near
        return a_all.at[s * 4 + yl_ * 2 + core_, lax.rem(y + k, NY)]

    def o_copy(k):
        c = chunk(0, yl, core, k)
        return remote(c, c, os.at[k], orr.at[k], row, outward)

    def x_copy(k, far=0):
        c = chunk(far, yl, core, k)
        return remote(c, c, xs.at[k], xr.at[k], row, across)

    def y_copy(far, k, yl_):
        c = chunk(far, yl_, core, k)
        return remote(c, c, ys.at[far, k], yr.at[far, k], row, y_mate)

    def c_copy(far, other, k, core_):
        c = chunk(far, 1 - yl if other else yl, core_, k)
        return remote(c, c, cs.at[far, other, k], cr.at[far, other, k], row, c_mate)

    def stage_a(k):
        @pl.when(hold == 1)
        def _():
            if k == 0:
                own_copy(0).wait()
            else:
                other = lax.rem(y + k, NY)
                remote(
                    a_ref.at[0], a_all.at[slot, other], a1s.at[0], a1r.at[other], row_at(1), col
                ).wait_recv()
            o_copy(k).start()

        @pl.when(hold == 0)
        def _():
            o_copy(k).wait_recv()

        x_copy(k).start()
        y_copy(0, k, yl).start()
        c_copy(0, 0, k, core).start()

    def stage_b(k):
        x_copy(k, 1).wait_recv()
        y_copy(1, k, yl).start()
        c_copy(1, 0, k, core).start()

    def stage_c(k):
        for far in range(2):
            y_copy(far, k, 1 - yl).wait_recv()
            c_copy(far, 1, k, core).start()

    stage_a(0)
    stage_a(1)
    f_step(1)
    stage_b(0)
    stage_a(3)
    stage_c(0)
    stage_b(1)
    stage_a(2)
    f_step(2)
    stage_c(1)
    stage_b(3)
    stage_b(2)
    f_step(3)
    stage_c(3)
    stage_c(2)
    f_step(4)
    for k in (0, 1, 3, 2):
        for other in range(2):
            for far in range(2):
                c_copy(far, other, k, 1 - core).wait_recv()

    y_up = lax.rem(y + 1, NY)
    y_down = lax.rem(y + NY - 1, NY)
    row_up, row_down = y_up * NZ + z, y_down * NZ + z

    def product(y_, k):
        left = jnp.concatenate([a_all[i, y_] for i in range(NZ)], axis=1)
        return mm(left, f_all[k].reshape(NZ * B, B))

    def pair(send, recv, ss, rs_, k):
        return (
            remote(send.at[k, 0], recv.at[k, 0], ss.at[k, 0], rs_.at[k, 0], row_up, col),
            remote(send.at[k, 1], recv.at[k, 1], ss.at[k, 1], rs_.at[k, 1], row_down, col),
        )

    def early(k):
        return pair(e_send, e_recv, es, er, k)

    def plain(k):
        return pair(p_send, p_recv, ps, pr, k)

    def grown(k):
        return pair(g_send, g_recv, gs, gr, k)

    bf = jnp.bfloat16
    for k in range(3):
        part = product(lax.rem(y + 2, NY), k).astype(bf)
        e_send[k, 0] = part[:half]
        e_send[k, 1] = part[half:]
        for copy in early(k):
            copy.start()
    for k in range(3):
        part = product(y_up, k)
        acc[0, k] = part[:half]
        p_send[k, 0] = part[half:].astype(bf)
        plain(k)[0].start()
        part = product(y_down, k)
        acc[1, k] = part[half:]
        p_send[k, 1] = part[:half].astype(bf)
        plain(k)[1].start()
    for k in range(3):
        for way in range(2):
            early(k)[way].wait_recv()
            g_send[k, way] = (acc[way, k] + e_recv[k, way].astype(jnp.float32)).astype(bf)
            grown(k)[way].start()
    for k in range(3):
        part = product(y, k)
        acc[2, k] = part[:half]
        acc[3, k] = part[half:]
    totals = []
    for k in range(3):
        for way in range(2):
            plain(k)[way].wait_recv()
            grown(k)[way].wait_recv()
        top = acc[2, k] + (g_recv[k, 0].astype(jnp.float32) + p_recv[k, 1].astype(jnp.float32))
        low_part = acc[3, k] + (p_recv[k, 0].astype(jnp.float32) + g_recv[k, 1].astype(jnp.float32))
        totals.append(jnp.concatenate([top, low_part], axis=0))

    second = par_ref[0] >= 16
    inv_a = (-totals[0] * m0).astype(bf)
    inv_b = (-totals[1] * m1).astype(bf)
    parent_cols = jnp.where(second, inv_b, inv_a)
    pb = pb_ref[...]
    side = mm(parent_cols, pb)
    inv_c = (-(totals[2] + side) * m2).astype(bf)
    inv1_ref[0] = inv_a
    inv1_ref[1] = inv_b
    inv2_ref[...] = inv_c
    per = B // SLICE

    def put(i, value):
        parts[pl.ds(i * per, per)] = value.astype(bf).reshape(per, SLICE, B)

    put(0, mm_t(f_all[0, z], inv_a))
    put(1, mm_t(f_all[1, z], inv_b))
    put(2, mm_t(parent_cols, f_all[2, z]))
    put(3, mm_t(f_all[2, z], inv_c))

    def first(d):
        return remote(parts.at[row_at(d)], r_recv.at[d], s1.at[d], r1.at[d], row_at(d), col)

    def second_copy(d):
        return remote(r_out.at[row], r_out.at[row], s2.at[d], r2.at[d], row_at(d), col)

    def loop(body):
        def step(d, carry):
            body(d)
            return carry

        lax.fori_loop(1, ROWS, step, 0)

    loop(lambda d: first(d).start())
    r_recv[0] = parts[row]
    loop(lambda d: first(d).wait_recv())
    r_out[row] = jnp.sum(r_recv[...].astype(jnp.float32), axis=0).astype(jnp.bfloat16)
    loop(lambda d: second_copy(d).start())
    loop(lambda d: second_copy(d).wait_recv())

    def block(i):
        return r_out[pl.ds(i * per, per)].reshape(B, B).astype(jnp.float32)

    diag_a = d1_ref[0] - block(0)
    diag_b = d1_ref[1] - block(1)
    diag1_ref[0] = diag_a
    diag1_ref[1] = diag_b
    parent_diag = jnp.where(second, diag_b, diag_a).astype(jnp.bfloat16)
    pinv = (-(mm(parent_diag, pb) + block(2))).astype(jnp.bfloat16)
    pinv_ref[...] = pinv
    diag2_ref[...] = d2_ref[...] - (block(3) + mm_t(pb, pinv))

    for k in range(3):
        for step in range(4):
            for copy in f_copies(step, k):
                copy.wait_send()
        for copies in (early(k), plain(k), grown(k)):
            for copy in copies:
                copy.wait_send()
    for h in range(2):

        @pl.when(2 * h + x // 2 != y)
        def _():
            a1_copy(h).wait_send()

    @pl.when(hold == 1)
    def _():
        for k in range(NY):
            o_copy(k).wait_send()

    for k in range(NY):
        x_copy(k).wait_send()
        for far in range(2):
            y_copy(far, k, yl).wait_send()
            for other in range(2):
                c_copy(far, other, k, core).wait_send()
    loop(lambda d: first(d).wait_send())
    loop(lambda d: second_copy(d).wait_send())


def body(anc, one, two, pb, d1, d2, p1, p2, par):
    a = anc.reshape(B, 2, B).transpose(1, 0, 2)
    f1 = one.reshape(B, 2, B).transpose(1, 0, 2)
    vmem = pl.BlockSpec(memory_space=pltpu.VMEM)
    smem = pl.BlockSpec(memory_space=pltpu.SMEM)
    dma = pltpu.SemaphoreType.DMA
    bf, f32 = jnp.bfloat16, jnp.float32
    inv1, diag1, inv2, pinv, diag2 = pl.pallas_call(
        kernel,
        out_shape=(
            jax.ShapeDtypeStruct((2, B, B), bf),
            jax.ShapeDtypeStruct((2, B, B), f32),
            jax.ShapeDtypeStruct((B, B), bf),
            jax.ShapeDtypeStruct((B, B), bf),
            jax.ShapeDtypeStruct((B, B), f32),
        ),
        in_specs=[smem] * 3 + [vmem] * 6,
        out_specs=(vmem,) * 5,
        scratch_shapes=[
            pltpu.VMEM((3, NZ, B, B), bf),
            pltpu.VMEM((NZ, NY, B, B), bf),
            pltpu.VMEM((4, 3, B // 2, B), f32),
        ]
        + [pltpu.VMEM((3, 2, B // 2, B), bf)] * 6
        + [pltpu.VMEM((ROWS, SLICE, B), bf)] * 3
        + [
            dma((2, 4, 3)), dma((2, 4, 3)),
            dma((2,)), dma((NY,)),
            dma((NY,)), dma((NY,)),
            dma((NY,)), dma((NY,)),
            dma((2, NY)), dma((2, NY)),
            dma((2, 2, NY)), dma((2, 2, NY)),
            dma((3, 2)), dma((3, 2)),
            dma((3, 2)), dma((3, 2)),
            dma((3, 2)), dma((3, 2)),
            dma((ROWS,)), dma((ROWS,)),
            dma((ROWS,)), dma((ROWS,)),
            dma(()),
        ],
        compiler_params=pltpu.CompilerParams(
            collective_id=0, has_side_effects=True, vmem_limit_bytes=40 * 1024 * 1024
        ),
    )(
        p1.reshape(2), p2.reshape(1), par.reshape(1), a, f1, two.reshape(B, B),
        pb.reshape(B, B), d1.reshape(2, B, B), d2.reshape(B, B),
    )
    return (
        inv1.transpose(1, 0, 2).reshape(one.shape),
        diag1.reshape(d1.shape),
        inv2.reshape(two.shape),
        pinv.reshape(pb.shape),
        diag2.reshape(d2.shape),
    )


def solution(mesh):
    placed = (
        P(None, "row", None, None, "col", None),
        P(None, "row", None, None, "col", None),
        P(None, "row", None, None, "col", None),
        P(None, "col", None, None),
        P(None, "col", None, None),
        P(None, "col", None, None),
        P(None, "row", None, "col"),
        P(None, "row", None, "col"),
        P(None, "col"),
    )
    return jax.shard_map(
        body,
        mesh=mesh,
        in_specs=placed,
        out_specs=(
            P(None, "row", None, None, "col", None),
            P(None, "col", None, None),
            P(None, "row", None, None, "col", None),
            P(None, "col", None, None),
            P(None, "col", None, None),
        ),
        check_vma=False,
    )
```

time: 159 us -> 130 us (0.82)
  the two profiles are of different devices: /device:TPU:2 before, /device:TPU:1 now
where the time goes in v2:
time: 130 us
  Pallas kernels  122 us (94%)
  local copies, waits for them, and re-layouts  5.64 us (4%)
  between operations  1.99 us (2%)
    pallas_call x1, Pallas kernels, body(): pl.pallas_call(kernel, out_shape=(jax.ShapeDtypeStruct((2, B, B), bf), ja...  122 us
    unnamed x15, local copies, waits for them, and re-layouts  4.45 us

profile of v2, /device:TPU:1, one launch (start us, length us, event | category | flops | bytes accessed | tf_op | source)
XLA Modules:
  0.0 130.1 jit_solution(7947593159154059449)
XLA Ops:
  1.9 0.0 copy-start
  1.9 0.0 copy-start.1
  1.9 0.0 copy-start.2
  2.0 0.0 copy-start.3
  2.0 1.2 copy_bitcast_fusion
  3.2 0.0 copy-start.4
  3.2 0.0 copy-done
  3.2 0.0 copy-done.1
  3.2 0.0 copy-done.2
  3.2 0.0 copy-done.3
  3.3 0.6 copy-done.4
  3.8 122.4 %shard_map.128 = (bf16[2,256,256]{2,1,0:T(8,128)(2,1)S(1)}, f32[2,256,256]{2,1,0:T(8,128)S(1)}, bf16[256,256]{1,0:T(8,128)(2,1)S(1)}, bf16[256,256]{1,0:T(8,128)(2,1)S(1)}, f32[256,256]{1,0:T(8,128)S(1)}) custom-call(s32[2]{0:T(128)S(1)} %bitcast.35, s32[1]{0:T(128)} %bitcast.24.p2_ref, s32[1]{0:T(128)} %bitcast.25.par_ref, ...), custom_call_target="tpu_custom_call" | custom-call | tf_op jit(solution)/shard_map/pallas_call | solution.py:335
  126.3 1.0 copy.16
  127.2 0.8 copy.26
  128.0 0.7 copy.27
  128.7 0.7 copy.28
  129.3 0.7 copy.29
Async XLA Ops:
  1.9 1.2 copy-start
  1.9 1.3 copy-start.1
  1.9 1.3 copy-start.2
  2.0 1.3 %copy-start.3 = (bf16[1,1,256,256]{3,2,1,0:T(8,128)(2,1)S(1)}, bf16[1,1,256,256]{3,2,1,0:T(8,128)(2,1)}, u32[]{:S(2)}) copy-start(bf16[1,1,256,256]{3,2,1,0:T(8,128)(2,1)} %param.12) | copy-start | bytes 393220
  3.2 0.7 copy-start.4

commit v3 on v2

--- a/solution.py
+++ b/solution.py
@@ -11,7 +11,7 @@
 B = 256
 NY, NZ, NX = 4, 8, 4
 ROWS = NY * NZ
-SLICE = 4 * B // ROWS
+SLICE = 2 * B // ROWS
 
 
 def mm(a, b):
@@ -25,8 +25,9 @@
 def kernel(
     p1_ref, p2_ref, par_ref, a_ref, f1_ref, f2_ref, pb_ref, d1_ref, d2_ref,
     inv1_ref, diag1_ref, inv2_ref, pinv_ref, diag2_ref,
-    f_all, a_all, acc, e_send, e_recv, p_send, p_recv, g_send, g_recv, parts, r_recv, r_out,
-    fs, fr, a1s, a1r, os, orr, xs, xr, ys, yr, cs, cr, es, er, ps, pr, gs, gr, s1, r1, s2, r2, own_sem,
+    f_all, a_all, acc, e_send, e_recv, p_send, p_recv, g_send, g_recv,
+    s0_part, s0_in, s0_mid, s0_mid_in, s0_out, s1_part, s1_in, s1_mid, s1_mid_in, s1_out,
+    fs, fr, a1s, a1r, os, orr, xs, xr, ys, yr, cs, cr, es, er, ps, pr, gs, gr, ss, sr, own_sem,
 ):
     row, col = lax.axis_index("row"), lax.axis_index("col")
     y, z = row // NZ, row % NZ
@@ -38,8 +39,11 @@
             device_id=(to_row, to_col), device_id_type=MESH,
         )
 
-    def row_at(d):
-        return lax.rem(row + d, ROWS)
+    def z_mate(d):
+        return y * NZ + lax.rem(z + d, NZ)
+
+    def y_row(d):
+        return lax.rem(y + d, NY) * NZ + z
 
     def col_of(x_, yl_, core_):
         return x_ * 4 + yl_ * 2 + core_
@@ -51,11 +55,8 @@
 
     barrier = pltpu.get_barrier_semaphore()
 
-    def greet(d, carry):
-        pl.semaphore_signal(barrier, inc=1, device_id=(row_at(d), col), device_id_type=MESH)
-        return carry
-
-    lax.fori_loop(1, ROWS, greet, 0)
+    for mate in [z_mate(d) for d in range(1, NZ)] + [y_row(d) for d in range(1, NY)]:
+        pl.semaphore_signal(barrier, inc=1, device_id=(mate, col), device_id_type=MESH)
     for mate in (across, outward, y_mate, c_mate):
         pl.semaphore_signal(barrier, inc=1, device_id=(row, mate), device_id_type=MESH)
     m0 = p1_ref[0].astype(jnp.float32)
@@ -64,7 +65,7 @@
     f_all[0, z] = f1_ref[0] * m0.astype(jnp.bfloat16)
     f_all[1, z] = f1_ref[1] * m1.astype(jnp.bfloat16)
     f_all[2, z] = f2_ref[...] * m2.astype(jnp.bfloat16)
-    pl.semaphore_wait(barrier, ROWS - 1 + 4)
+    pl.semaphore_wait(barrier, NZ - 1 + NY - 1 + 4)
 
     up = y * NZ + lax.rem(z + 1, NZ)
     down = y * NZ + lax.rem(z + NZ - 1, NZ)
@@ -145,7 +146,7 @@
             else:
                 other = lax.rem(y + k, NY)
                 remote(
-                    a_ref.at[0], a_all.at[slot, other], a1s.at[0], a1r.at[other], row_at(1), col
+                    a_ref.at[0], a_all.at[slot, other], a1s.at[0], a1r.at[other], y_row(1), col
                 ).wait_recv()
             o_copy(k).start()
 
@@ -211,14 +212,9 @@
     def grown(k):
         return pair(g_send, g_recv, gs, gr, k)
 
-    bf = jnp.bfloat16
-    for k in range(3):
-        part = product(lax.rem(y + 2, NY), k).astype(bf)
-        e_send[k, 0] = part[:half]
-        e_send[k, 1] = part[half:]
-        for copy in early(k):
-            copy.start()
-    for k in range(3):
+    bf, f32 = jnp.bfloat16, jnp.float32
+
+    def send_plain(k):
         part = product(y_up, k)
         acc[0, k] = part[:half]
         p_send[k, 0] = part[half:].astype(bf)
@@ -227,75 +223,125 @@
         acc[1, k] = part[half:]
         p_send[k, 1] = part[:half].astype(bf)
         plain(k)[1].start()
-    for k in range(3):
+
+    def send_grown(k):
         for way in range(2):
             early(k)[way].wait_recv()
-            g_send[k, way] = (acc[way, k] + e_recv[k, way].astype(jnp.float32)).astype(bf)
+            g_send[k, way] = (acc[way, k] + e_recv[k, way].astype(f32)).astype(bf)
             grown(k)[way].start()
+
+    def total(k):
+        for way in range(2):
+            plain(k)[way].wait_recv()
+            grown(k)[way].wait_recv()
+        top = acc[2, k] + (g_recv[k, 0].astype(f32) + p_recv[k, 1].astype(f32))
+        bottom = acc[3, k] + (p_recv[k, 0].astype(f32) + g_recv[k, 1].astype(f32))
+        return jnp.concatenate([top, bottom], axis=0)
+
+    for k in range(3):
+        part = product(lax.rem(y + 2, NY), k).astype(bf)
+        e_send[k, 0] = part[:half]
+        e_send[k, 1] = part[half:]
+        for copy in early(k):
+            copy.start()
+    send_plain(0)
+    send_plain(1)
+    send_grown(0)
+    send_grown(1)
+    send_plain(2)
+    send_grown(2)
     for k in range(3):
         part = product(y, k)
         acc[2, k] = part[:half]
         acc[3, k] = part[half:]
-    totals = []
-    for k in range(3):
-        for way in range(2):
-            plain(k)[way].wait_recv()
-            grown(k)[way].wait_recv()
-        top = acc[2, k] + (g_recv[k, 0].astype(jnp.float32) + p_recv[k, 1].astype(jnp.float32))
-        low_part = acc[3, k] + (p_recv[k, 0].astype(jnp.float32) + g_recv[k, 1].astype(jnp.float32))
-        totals.append(jnp.concatenate([top, low_part], axis=0))
+
+    def over_z(stage, src, dst):
+        return [
+            remote(src(d), dst(d), ss.at[stage, d], sr.at[stage, d], z_mate(d), col) for d in range(1, NZ)
+        ]
+
+    def over_y(stage, src, dst):
+        return [
+            remote(src(d), dst(d), ss.at[stage, d], sr.at[stage, d], y_row(d), col) for d in range(1, NY)
+        ]
+
+    def z_at(d):
+        return lax.rem(z + d, NZ)
+
+    def y_at(d):
+        return lax.rem(y + d, NY)
+
+    stages = (
+        lambda: over_z(0, lambda d: s0_part.at[z_at(d)], lambda d: s0_in.at[d]),
+        lambda: over_y(1, lambda d: s1_part.at[y_at(d)], lambda d: s1_in.at[d]),
+        lambda: over_y(2, lambda d: s0_mid.at[y_at(d)], lambda d: s0_mid_in.at[d]),
+        lambda: over_z(3, lambda d: s1_mid.at[z_at(d)], lambda d: s1_mid_in.at[d]),
+        lambda: over_y(4, lambda d: s0_out.at[z, y], lambda d: s0_out.at[z, y]),
+        lambda: over_z(5, lambda d: s1_out.at[y, z], lambda d: s1_out.at[y, z]),
+        lambda: over_z(6, lambda d: s0_out.at[z], lambda d: s0_out.at[z]),
+        lambda: over_y(7, lambda d: s1_out.at[y], lambda d: s1_out.at[y]),
+    )
+
+    def start(stage):
+        for copy in stages[stage]():
+            copy.start()
+
+    def arrived(stage):
+        for copy in stages[stage]():
+            copy.wait_recv()
+
+    def added(ref):
+        return jnp.sum(ref[...].astype(f32), axis=0).astype(bf)
 
     second = par_ref[0] >= 16
-    inv_a = (-totals[0] * m0).astype(bf)
-    inv_b = (-totals[1] * m1).astype(bf)
+    inv_a = (-total(0) * m0).astype(bf)
+    inv_b = (-total(1) * m1).astype(bf)
+    s0_part[pl.ds(0, NZ // 2)] = mm_t(f_all[0, z], inv_a).astype(bf).reshape(NZ // 2, NY * SLICE, B)
+    s0_part[pl.ds(NZ // 2, NZ // 2)] = mm_t(f_all[1, z], inv_b).astype(bf).reshape(NZ // 2, NY * SLICE, B)
+    start(0)
+    s0_in[0] = s0_part[z]
     parent_cols = jnp.where(second, inv_b, inv_a)
     pb = pb_ref[...]
     side = mm(parent_cols, pb)
-    inv_c = (-(totals[2] + side) * m2).astype(bf)
+    s1_part[pl.ds(0, NY // 2)] = mm_t(parent_cols, f_all[2, z]).astype(bf).reshape(NY // 2, NZ * SLICE, B)
+    inv_c = (-(total(2) + side) * m2).astype(bf)
+    s1_part[pl.ds(NY // 2, NY // 2)] = mm_t(f_all[2, z], inv_c).astype(bf).reshape(NY // 2, NZ * SLICE, B)
+    start(1)
+    s1_in[0] = s1_part[y]
     inv1_ref[0] = inv_a
     inv1_ref[1] = inv_b
     inv2_ref[...] = inv_c
-    per = B // SLICE
-
-    def put(i, value):
-        parts[pl.ds(i * per, per)] = value.astype(bf).reshape(per, SLICE, B)
-
-    put(0, mm_t(f_all[0, z], inv_a))
-    put(1, mm_t(f_all[1, z], inv_b))
-    put(2, mm_t(parent_cols, f_all[2, z]))
-    put(3, mm_t(f_all[2, z], inv_c))
-
-    def first(d):
-        return remote(parts.at[row_at(d)], r_recv.at[d], s1.at[d], r1.at[d], row_at(d), col)
-
-    def second_copy(d):
-        return remote(r_out.at[row], r_out.at[row], s2.at[d], r2.at[d], row_at(d), col)
-
-    def loop(body):
-        def step(d, carry):
-            body(d)
-            return carry
-
-        lax.fori_loop(1, ROWS, step, 0)
-
-    loop(lambda d: first(d).start())
-    r_recv[0] = parts[row]
-    loop(lambda d: first(d).wait_recv())
-    r_out[row] = jnp.sum(r_recv[...].astype(jnp.float32), axis=0).astype(jnp.bfloat16)
-    loop(lambda d: second_copy(d).start())
-    loop(lambda d: second_copy(d).wait_recv())
-
-    def block(i):
-        return r_out[pl.ds(i * per, per)].reshape(B, B).astype(jnp.float32)
-
-    diag_a = d1_ref[0] - block(0)
-    diag_b = d1_ref[1] - block(1)
+    arrived(0)
+    s0_mid[...] = added(s0_in).reshape(NY, SLICE, B)
+    start(2)
+    s0_mid_in[0] = s0_mid[y]
+    arrived(1)
+    s1_mid[...] = added(s1_in).reshape(NZ, SLICE, B)
+    start(3)
+    s1_mid_in[0] = s1_mid[z]
+    arrived(2)
+    s0_out[z, y] = added(s0_mid_in)
+    start(4)
+    arrived(3)
+    s1_out[y, z] = added(s1_mid_in)
+    start(5)
+    arrived(4)
+    start(6)
+    arrived(5)
+    start(7)
+    arrived(6)
+    diag_sum = s0_out[...].reshape(2, B, B).astype(f32)
+    diag_a = d1_ref[0] - diag_sum[0]
+    diag_b = d1_ref[1] - diag_sum[1]
     diag1_ref[0] = diag_a
     diag1_ref[1] = diag_b
-    parent_diag = jnp.where(second, diag_b, diag_a).astype(jnp.bfloat16)
-    pinv = (-(mm(parent_diag, pb) + block(2))).astype(jnp.bfloat16)
+    parent_diag = jnp.where(second, diag_b, diag_a).astype(bf)
+    ahead = mm(parent_diag, pb)
+    arrived(7)
+    other_sum = s1_out[...].reshape(2, B, B).astype(f32)
+    pinv = (-(ahead + other_sum[0])).astype(bf)
     pinv_ref[...] = pinv
-    diag2_ref[...] = d2_ref[...] - (block(3) + mm_t(pb, pinv))
+    diag2_ref[...] = d2_ref[...] - (other_sum[1] + mm_t(pb, pinv))
 
     for k in range(3):
         for step in range(4):
@@ -321,8 +367,9 @@
             y_copy(far, k, yl).wait_send()
             for other in range(2):
                 c_copy(far, other, k, core).wait_send()
-    loop(lambda d: first(d).wait_send())
-    loop(lambda d: second_copy(d).wait_send())
+    for stage in stages:
+        for copy in stage():
+            copy.wait_send()
 
 
 def body(anc, one, two, pb, d1, d2, p1, p2, par):
@@ -349,7 +396,14 @@
             pltpu.VMEM((4, 3, B // 2, B), f32),
         ]
         + [pltpu.VMEM((3, 2, B // 2, B), bf)] * 6
-        + [pltpu.VMEM((ROWS, SLICE, B), bf)] * 3
+        + [
+            pltpu.VMEM((NZ, NY * SLICE, B), bf), pltpu.VMEM((NZ, NY * SLICE, B), bf),
+            pltpu.VMEM((NY, SLICE, B), bf), pltpu.VMEM((NY, SLICE, B), bf),
+            pltpu.VMEM((NZ, NY, SLICE, B), bf),
+            pltpu.VMEM((NY, NZ * SLICE, B), bf), pltpu.VMEM((NY, NZ * SLICE, B), bf),
+            pltpu.VMEM((NZ, SLICE, B), bf), pltpu.VMEM((NZ, SLICE, B), bf),
+            pltpu.VMEM((NY, NZ, SLICE, B), bf),
+        ]
         + [
             dma((2, 4, 3)), dma((2, 4, 3)),
             dma((2,)), dma((NY,)),
@@ -360,8 +414,7 @@
             dma((3, 2)), dma((3, 2)),
             dma((3, 2)), dma((3, 2)),
             dma((3, 2)), dma((3, 2)),
-            dma((ROWS,)), dma((ROWS,)),
-            dma((ROWS,)), dma((ROWS,)),
+            dma((8, NZ)), dma((8, NZ)),
             dma(()),
         ],
         compiler_params=pltpu.CompilerParams(

time: 130 us -> 119 us (0.915); the launches traced: 130 us -> 117 us
  Pallas kernels: 122 us -> 109 us
    pallas_call x1, Pallas kernels: 122 us -> 109 us  [body(): pl.pallas_call(kernel, out_shape=(jax.ShapeDtypeStruct((2, B, B), bf), ja...]
where the time goes in v3:
time: 119 us; the launch traced here: 117 us
  Pallas kernels  109 us (92%)
  local copies, waits for them, and re-layouts  5.64 us (5%)
  between operations  1.99 us (2%)
    pallas_call x1, Pallas kernels, body(): pl.pallas_call(kernel, out_shape=(jax.ShapeDtypeStruct((2, B, B), bf), ja...  109 us
    unnamed x15, local copies, waits for them, and re-layouts  4.45 us

profile of v3, /device:TPU:1, one launch (start us, length us, event | category | flops | bytes accessed | tf_op | source)
XLA Modules:
  0.0 117.0 jit_solution(3674703664619659852)
XLA Ops:
  1.9 0.0 copy-start
  1.9 0.0 copy-start.1
  1.9 0.0 copy-start.2
  2.0 0.0 copy-start.3
  2.0 1.2 %copy_bitcast_fusion = (bf16[2,256,256]{2,1,0:T(8,128)(2,1)S(1)}, bf16[2,256,256]{2,1,0:T(8,128)(2,1)S(1)}) fusion(bf16[1,1,256,2,1,256]{5,3,4,2,1,0:T(2,128)(2,1)} %param.10, bf16[1,1,256,2,1,256]{5,3,4,2,1,0:T(2,128)(2,1)} %param.9), kind=kLoop, calls=%fused_computation | loop fusion | bytes 1048576 | tf_op jit(solution)/shard_map/transpose | solution.py:377
  3.2 0.0 copy-start.4
  3.2 0.0 copy-done
  3.2 0.0 copy-done.1
  3.2 0.0 copy-done.2
  3.2 0.0 copy-done.3
  3.3 0.6 copy-done.4
  3.8 109.3 %shard_map.128 = (bf16[2,256,256]{2,1,0:T(8,128)(2,1)S(1)}, f32[2,256,256]{2,1,0:T(8,128)S(1)}, bf16[256,256]{1,0:T(8,128)(2,1)S(1)}, bf16[256,256]{1,0:T(8,128)(2,1)S(1)}, f32[256,256]{1,0:T(8,128)S(1)}) custom-call(s32[2]{0:T(128)S(1)} %bitcast.35, s32[1]{0:T(128)} %bitcast.24.p2_ref, s32[1]{0:T(128)} %bitcast.25.par_ref, ...), custom_call_target="tpu_custom_call" | custom-call | tf_op jit(solution)/shard_map/pallas_call | solution.py:382
  113.2 1.0 copy.16
  114.2 0.8 copy.26
  114.9 0.7 copy.27
  115.6 0.7 copy.28
  116.3 0.7 copy.29
Async XLA Ops:
  1.9 1.2 %copy-start = (f32[2,1,256,256]{3,2,1,0:T(8,128)S(1)}, f32[2,1,256,256]{3,2,1,0:T(8,128)}, u32[]{:S(2)}) copy-start(f32[2,1,256,256]{3,2,1,0:T(8,128)} %param.13) | copy-start | bytes 1572868
  1.9 1.3 %copy-start.1 = (f32[1,1,256,256]{3,2,1,0:T(8,128)S(1)}, f32[1,1,256,256]{3,2,1,0:T(8,128)}, u32[]{:S(2)}) copy-start(f32[1,1,256,256]{3,2,1,0:T(8,128)} %param.14) | copy-start | bytes 786436
  1.9 1.3 %copy-start.2 = (bf16[1,1,256,1,1,256]{5,2,4,3,1,0:T(8,128)(2,1)S(1)}, bf16[1,1,256,1,1,256]{5,2,4,3,1,0:T(8,128)(2,1)}, u32[]{:S(2)}) copy-start(bf16[1,1,256,1,1,256]{5,2,4,3,1,0:T(8,128)(2,1)} %param.11) | copy-start | bytes 393220
  2.0 1.3 %copy-start.3 = (bf16[1,1,256,256]{3,2,1,0:T(8,128)(2,1)S(1)}, bf16[1,1,256,256]{3,2,1,0:T(8,128)(2,1)}, u32[]{:S(2)}) copy-start(bf16[1,1,256,256]{3,2,1,0:T(8,128)(2,1)} %param.12) | copy-start | bytes 393220
  3.2 0.7 copy-start.4

commit v4 on v3

--- a/solution.py
+++ b/solution.py
@@ -10,8 +10,7 @@
 MESH = pl.DeviceIdType.MESH
 B = 256
 NY, NZ, NX = 4, 8, 4
-ROWS = NY * NZ
-SLICE = 2 * B // ROWS
+SLICE = B // NZ
 
 
 def mm(a, b):
@@ -26,7 +25,7 @@
     p1_ref, p2_ref, par_ref, a_ref, f1_ref, f2_ref, pb_ref, d1_ref, d2_ref,
     inv1_ref, diag1_ref, inv2_ref, pinv_ref, diag2_ref,
     f_all, a_all, acc, e_send, e_recv, p_send, p_recv, g_send, g_recv,
-    s0_part, s0_in, s0_mid, s0_mid_in, s0_out, s1_part, s1_in, s1_mid, s1_mid_in, s1_out,
+    s0_part, s0_in, s0_mid, s0_out, s1_part, s1_in, s1_mid, s1_out,
     fs, fr, a1s, a1r, os, orr, xs, xr, ys, yr, cs, cr, es, er, ps, pr, gs, gr, ss, sr, own_sem,
 ):
     row, col = lax.axis_index("row"), lax.axis_index("col")
@@ -84,14 +83,13 @@
             remote(d, d, fs.at[1, step, k], fr.at[1, step, k], down, col),
         )
 
-    def f_step(step):
-        for k in range(3):
-            if step > 0:
-                for copy in f_copies(step - 1, k):
-                    copy.wait_recv()
-            if step < 4:
-                for copy in f_copies(step, k):
-                    copy.start()
+    def f_step(k, step):
+        if step > 0:
+            for copy in f_copies(step - 1, k):
+                copy.wait_recv()
+        if step < 4:
+            for copy in f_copies(step, k):
+                copy.start()
 
     slot = lax.rem(col, NZ)
     hold = lax.rem(y + x // 2 + 1, 2)
@@ -116,29 +114,27 @@
         def _():
             own_copy(h).start()
 
-    f_step(0)
-
     def chunk(far, yl_, core_, k):
         s = 1 - near if far else near
         return a_all.at[s * 4 + yl_ * 2 + core_, lax.rem(y + k, NY)]
 
-    def o_copy(k):
-        c = chunk(0, yl, core, k)
-        return remote(c, c, os.at[k], orr.at[k], row, outward)
-
-    def x_copy(k, far=0):
-        c = chunk(far, yl, core, k)
-        return remote(c, c, xs.at[k], xr.at[k], row, across)
-
-    def y_copy(far, k, yl_):
-        c = chunk(far, yl_, core, k)
-        return remote(c, c, ys.at[far, k], yr.at[far, k], row, y_mate)
+    def y_copy(k, yl_):
+        c = chunk(0, yl_, core, k)
+        return remote(c, c, ys.at[k], yr.at[k], row, y_mate)
+
+    def o_copy(other, k):
+        c = chunk(0, 1 - yl if other else yl, core, k)
+        return remote(c, c, os.at[other, k], orr.at[other, k], row, outward)
+
+    def x_copy(other, k, far=0):
+        c = chunk(far, 1 - yl if other else yl, core, k)
+        return remote(c, c, xs.at[other, k], xr.at[other, k], row, across)
 
     def c_copy(far, other, k, core_):
         c = chunk(far, 1 - yl if other else yl, core_, k)
         return remote(c, c, cs.at[far, other, k], cr.at[far, other, k], row, c_mate)
 
-    def stage_a(k):
+    def near_own(k):
         @pl.when(hold == 1)
         def _():
             if k == 0:
@@ -148,45 +144,37 @@
                 remote(
                     a_ref.at[0], a_all.at[slot, other], a1s.at[0], a1r.at[other], y_row(1), col
                 ).wait_recv()
-            o_copy(k).start()
+            y_copy(k, yl).start()
+            o_copy(0, k).start()
 
         @pl.when(hold == 0)
         def _():
-            o_copy(k).wait_recv()
-
-        x_copy(k).start()
-        y_copy(0, k, yl).start()
+            o_copy(0, k).wait_recv()
+
+        x_copy(0, k).start()
         c_copy(0, 0, k, core).start()
 
-    def stage_b(k):
-        x_copy(k, 1).wait_recv()
-        y_copy(1, k, yl).start()
-        c_copy(1, 0, k, core).start()
-
-    def stage_c(k):
+    def near_other(k):
+        @pl.when(hold == 1)
+        def _():
+            y_copy(k, 1 - yl).wait_recv()
+            o_copy(1, k).start()
+
+        @pl.when(hold == 0)
+        def _():
+            o_copy(1, k).wait_recv()
+
+        x_copy(1, k).start()
+        c_copy(0, 1, k, core).start()
+
+    def far_both(k):
+        for other in range(2):
+            x_copy(other, k, 1).wait_recv()
+            c_copy(1, other, k, core).start()
+
+    def whole(k):
         for far in range(2):
-            y_copy(far, k, 1 - yl).wait_recv()
-            c_copy(far, 1, k, core).start()
-
-    stage_a(0)
-    stage_a(1)
-    f_step(1)
-    stage_b(0)
-    stage_a(3)
-    stage_c(0)
-    stage_b(1)
-    stage_a(2)
-    f_step(2)
-    stage_c(1)
-    stage_b(3)
-    stage_b(2)
-    f_step(3)
-    stage_c(3)
-    stage_c(2)
-    f_step(4)
-    for k in (0, 1, 3, 2):
-        for other in range(2):
-            for far in range(2):
+            for other in range(2):
                 c_copy(far, other, k, 1 - core).wait_recv()
 
     y_up = lax.rem(y + 1, NY)
@@ -214,15 +202,29 @@
 
     bf, f32 = jnp.bfloat16, jnp.float32
 
-    def send_plain(k):
+    def send_early(k):
+        part = product(lax.rem(y + 2, NY), k).astype(bf)
+        e_send[k, 0] = part[:half]
+        e_send[k, 1] = part[half:]
+        for copy in early(k):
+            copy.start()
+
+    def send_up(k):
         part = product(y_up, k)
         acc[0, k] = part[:half]
         p_send[k, 0] = part[half:].astype(bf)
         plain(k)[0].start()
+
+    def send_down(k):
         part = product(y_down, k)
         acc[1, k] = part[half:]
         p_send[k, 1] = part[:half].astype(bf)
         plain(k)[1].start()
+
+    def own(k):
+        part = product(y, k)
+        acc[2, k] = part[:half]
+        acc[3, k] = part[half:]
 
     def send_grown(k):
         for way in range(2):
@@ -238,22 +240,51 @@
         bottom = acc[3, k] + (p_recv[k, 0].astype(f32) + g_recv[k, 1].astype(f32))
         return jnp.concatenate([top, bottom], axis=0)
 
-    for k in range(3):
-        part = product(lax.rem(y + 2, NY), k).astype(bf)
-        e_send[k, 0] = part[:half]
-        e_send[k, 1] = part[half:]
-        for copy in early(k):
-            copy.start()
-    send_plain(0)
-    send_plain(1)
+    f_step(0, 0)
+    f_step(1, 0)
+    near_own(0)
+    f_step(0, 1)
+    near_other(0)
+    f_step(1, 1)
+    near_own(2)
+    far_both(0)
+    f_step(0, 2)
+    near_own(1)
+    near_other(2)
+    f_step(1, 2)
+    near_own(3)
+    far_both(2)
+    near_other(1)
+    f_step(0, 3)
+    f_step(2, 0)
+    f_step(1, 3)
+    near_other(3)
+    far_both(1)
+    whole(2)
+    f_step(2, 1)
+    f_step(0, 4)
+    send_early(0)
+    f_step(1, 4)
+    send_early(1)
+    far_both(3)
+    whole(1)
+    f_step(2, 2)
+    send_up(0)
+    send_up(1)
+    whole(3)
+    send_down(0)
+    send_down(1)
+    f_step(2, 3)
     send_grown(0)
     send_grown(1)
-    send_plain(2)
-    send_grown(2)
-    for k in range(3):
-        part = product(y, k)
-        acc[2, k] = part[:half]
-        acc[3, k] = part[half:]
+    whole(0)
+    own(0)
+    own(1)
+    f_step(2, 4)
+    send_early(2)
+    send_up(2)
+    send_down(2)
+    own(2)
 
     def over_z(stage, src, dst):
         return [
@@ -268,18 +299,13 @@
     def z_at(d):
         return lax.rem(z + d, NZ)
 
-    def y_at(d):
-        return lax.rem(y + d, NY)
-
     stages = (
         lambda: over_z(0, lambda d: s0_part.at[z_at(d)], lambda d: s0_in.at[d]),
-        lambda: over_y(1, lambda d: s1_part.at[y_at(d)], lambda d: s1_in.at[d]),
-        lambda: over_y(2, lambda d: s0_mid.at[y_at(d)], lambda d: s0_mid_in.at[d]),
-        lambda: over_z(3, lambda d: s1_mid.at[z_at(d)], lambda d: s1_mid_in.at[d]),
-        lambda: over_y(4, lambda d: s0_out.at[z, y], lambda d: s0_out.at[z, y]),
-        lambda: over_z(5, lambda d: s1_out.at[y, z], lambda d: s1_out.at[y, z]),
-        lambda: over_z(6, lambda d: s0_out.at[z], lambda d: s0_out.at[z]),
-        lambda: over_y(7, lambda d: s1_out.at[y], lambda d: s1_out.at[y]),
+        lambda: over_z(1, lambda d: s1_part.at[z_at(d)], lambda d: s1_in.at[d]),
+        lambda: over_y(2, lambda d: s0_mid.at[y], lambda d: s0_mid.at[y]),
+        lambda: over_y(3, lambda d: s1_mid.at[y], lambda d: s1_mid.at[y]),
+        lambda: over_z(4, lambda d: s0_out.at[z], lambda d: s0_out.at[z]),
+        lambda: over_z(5, lambda d: s1_out.at[z], lambda d: s1_out.at[z]),
     )
 
     def start(stage):
@@ -296,52 +322,47 @@
     second = par_ref[0] >= 16
     inv_a = (-total(0) * m0).astype(bf)
     inv_b = (-total(1) * m1).astype(bf)
-    s0_part[pl.ds(0, NZ // 2)] = mm_t(f_all[0, z], inv_a).astype(bf).reshape(NZ // 2, NY * SLICE, B)
-    s0_part[pl.ds(NZ // 2, NZ // 2)] = mm_t(f_all[1, z], inv_b).astype(bf).reshape(NZ // 2, NY * SLICE, B)
+    parent_cols = jnp.where(second, inv_b, inv_a)
+    level_one = jnp.concatenate(
+        [mm_t(f_all[0, z], inv_a), mm_t(f_all[1, z], inv_b), mm_t(parent_cols, f_all[2, z])], axis=0
+    )
+    s0_part[...] = level_one.astype(bf).reshape(NZ, 3 * SLICE, B)
     start(0)
+    send_grown(2)
     s0_in[0] = s0_part[z]
-    parent_cols = jnp.where(second, inv_b, inv_a)
     pb = pb_ref[...]
     side = mm(parent_cols, pb)
-    s1_part[pl.ds(0, NY // 2)] = mm_t(parent_cols, f_all[2, z]).astype(bf).reshape(NY // 2, NZ * SLICE, B)
-    inv_c = (-(total(2) + side) * m2).astype(bf)
-    s1_part[pl.ds(NY // 2, NY // 2)] = mm_t(f_all[2, z], inv_c).astype(bf).reshape(NY // 2, NZ * SLICE, B)
-    start(1)
-    s1_in[0] = s1_part[y]
     inv1_ref[0] = inv_a
     inv1_ref[1] = inv_b
+    inv_c = (-(total(2) + side) * m2).astype(bf)
+    s1_part[...] = mm_t(f_all[2, z], inv_c).astype(bf).reshape(NZ, SLICE, B)
+    start(1)
+    s1_in[0] = s1_part[z]
     inv2_ref[...] = inv_c
     arrived(0)
-    s0_mid[...] = added(s0_in).reshape(NY, SLICE, B)
+    s0_mid[y] = added(s0_in)
     start(2)
-    s0_mid_in[0] = s0_mid[y]
     arrived(1)
-    s1_mid[...] = added(s1_in).reshape(NZ, SLICE, B)
+    s1_mid[y] = added(s1_in)
     start(3)
-    s1_mid_in[0] = s1_mid[z]
     arrived(2)
-    s0_out[z, y] = added(s0_mid_in)
+    s0_out[z] = added(s0_mid)
     start(4)
     arrived(3)
-    s1_out[y, z] = added(s1_mid_in)
+    s1_out[z] = added(s1_mid)
     start(5)
     arrived(4)
-    start(6)
-    arrived(5)
-    start(7)
-    arrived(6)
-    diag_sum = s0_out[...].reshape(2, B, B).astype(f32)
-    diag_a = d1_ref[0] - diag_sum[0]
-    diag_b = d1_ref[1] - diag_sum[1]
+    sums = s0_out[...].reshape(3, B, B).astype(f32)
+    diag_a = d1_ref[0] - sums[0]
+    diag_b = d1_ref[1] - sums[1]
     diag1_ref[0] = diag_a
     diag1_ref[1] = diag_b
     parent_diag = jnp.where(second, diag_b, diag_a).astype(bf)
-    ahead = mm(parent_diag, pb)
-    arrived(7)
-    other_sum = s1_out[...].reshape(2, B, B).astype(f32)
-    pinv = (-(ahead + other_sum[0])).astype(bf)
+    pinv = (-(mm(parent_diag, pb) + sums[2])).astype(bf)
     pinv_ref[...] = pinv
-    diag2_ref[...] = d2_ref[...] - (other_sum[1] + mm_t(pb, pinv))
+    ahead = d2_ref[...] - mm_t(pb, pinv)
+    arrived(5)
+    diag2_ref[...] = ahead - s1_out[...].reshape(B, B).astype(f32)
 
     for k in range(3):
         for step in range(4):
@@ -359,13 +380,14 @@
     @pl.when(hold == 1)
     def _():
         for k in range(NY):
-            o_copy(k).wait_send()
+            y_copy(k, yl).wait_send()
+            for other in range(2):
+                o_copy(other, k).wait_send()
 
     for k in range(NY):
-        x_copy(k).wait_send()
-        for far in range(2):
-            y_copy(far, k, yl).wait_send()
-            for other in range(2):
+        for other in range(2):
+            x_copy(other, k).wait_send()
+            for far in range(2):
                 c_copy(far, other, k, core).wait_send()
     for stage in stages:
         for copy in stage():
@@ -397,24 +419,22 @@
         ]
         + [pltpu.VMEM((3, 2, B // 2, B), bf)] * 6
         + [
-            pltpu.VMEM((NZ, NY * SLICE, B), bf), pltpu.VMEM((NZ, NY * SLICE, B), bf),
-            pltpu.VMEM((NY, SLICE, B), bf), pltpu.VMEM((NY, SLICE, B), bf),
-            pltpu.VMEM((NZ, NY, SLICE, B), bf),
-            pltpu.VMEM((NY, NZ * SLICE, B), bf), pltpu.VMEM((NY, NZ * SLICE, B), bf),
+            pltpu.VMEM((NZ, 3 * SLICE, B), bf), pltpu.VMEM((NZ, 3 * SLICE, B), bf),
+            pltpu.VMEM((NY, 3 * SLICE, B), bf), pltpu.VMEM((NZ, 3 * SLICE, B), bf),
             pltpu.VMEM((NZ, SLICE, B), bf), pltpu.VMEM((NZ, SLICE, B), bf),
-            pltpu.VMEM((NY, NZ, SLICE, B), bf),
+            pltpu.VMEM((NY, SLICE, B), bf), pltpu.VMEM((NZ, SLICE, B), bf),
         ]
         + [
             dma((2, 4, 3)), dma((2, 4, 3)),
             dma((2,)), dma((NY,)),
+            dma((2, NY)), dma((2, NY)),
+            dma((2, NY)), dma((2, NY)),
             dma((NY,)), dma((NY,)),
-            dma((NY,)), dma((NY,)),
-            dma((2, NY)), dma((2, NY)),
             dma((2, 2, NY)), dma((2, 2, NY)),
             dma((3, 2)), dma((3, 2)),
             dma((3, 2)), dma((3, 2)),
             dma((3, 2)), dma((3, 2)),
-            dma((8, NZ)), dma((8, NZ)),
+            dma((6, NZ)), dma((6, NZ)),
             dma(()),
         ],
         compiler_params=pltpu.CompilerParams(

time: 119 us -> 109 us (0.916)
  the two profiles are of different devices: /device:TPU:1 before, /device:TPU:8 now
where the time goes in v4:
time: 109 us
  Pallas kernels  102 us (94%)
  local copies, waits for them, and re-layouts  5.64 us (5%)
  between operations  1.99 us (2%)
    pallas_call x1, Pallas kernels, body(): pl.pallas_call(kernel, out_shape=(jax.ShapeDtypeStruct((2, B, B), bf), ja...  102 us
    unnamed x15, local copies, waits for them, and re-layouts  4.45 us

profile of v4, /device:TPU:8, one launch (start us, length us, event | category | flops | bytes accessed | tf_op | source)
XLA Modules:
  0.0 109.1 jit_solution(11856441985672281726)
XLA Ops:
  1.9 0.0 copy-start
  1.9 0.0 copy-start.1
  1.9 0.0 copy-start.2
  2.0 0.0 copy-start.3
  2.0 1.2 %copy_bitcast_fusion = (bf16[2,256,256]{2,1,0:T(8,128)(2,1)S(1)}, bf16[2,256,256]{2,1,0:T(8,128)(2,1)S(1)}) fusion(bf16[1,1,256,2,1,256]{5,3,4,2,1,0:T(2,128)(2,1)} %param.10, bf16[1,1,256,2,1,256]{5,3,4,2,1,0:T(2,128)(2,1)} %param.9), kind=kLoop, calls=%fused_computation | loop fusion | bytes 1048576 | tf_op jit(solution)/shard_map/transpose | solution.py:399
  3.2 0.0 copy-start.4
  3.2 0.0 copy-done
  3.2 0.0 copy-done.1
  3.2 0.0 copy-done.2
  3.2 0.0 copy-done.3
  3.3 0.6 copy-done.4
  3.8 101.5 %shard_map.128 = (bf16[2,256,256]{2,1,0:T(8,128)(2,1)S(1)}, f32[2,256,256]{2,1,0:T(8,128)S(1)}, bf16[256,256]{1,0:T(8,128)(2,1)S(1)}, bf16[256,256]{1,0:T(8,128)(2,1)S(1)}, f32[256,256]{1,0:T(8,128)S(1)}) custom-call(s32[2]{0:T(128)S(1)} %bitcast.35, s32[1]{0:T(128)} %bitcast.24.p2_ref, s32[1]{0:T(128)} %bitcast.25.par_ref, ...), custom_call_target="tpu_custom_call" | custom-call | tf_op jit(solution)/shard_map/pallas_call | solution.py:404
  105.4 1.0 copy.16
  106.3 0.8 copy.26
  107.1 0.7 copy.27
  107.8 0.7 copy.28
  108.4 0.7 copy.29
Async XLA Ops:
  1.9 1.2 %copy-start = (f32[2,1,256,256]{3,2,1,0:T(8,128)S(1)}, f32[2,1,256,256]{3,2,1,0:T(8,128)}, u32[]{:S(2)}) copy-start(f32[2,1,256,256]{3,2,1,0:T(8,128)} %param.13) | copy-start | bytes 1572868
  1.9 1.3 %copy-start.1 = (f32[1,1,256,256]{3,2,1,0:T(8,128)S(1)}, f32[1,1,256,256]{3,2,1,0:T(8,128)}, u32[]{:S(2)}) copy-start(f32[1,1,256,256]{3,2,1,0:T(8,128)} %param.14) | copy-start | bytes 786436
  1.9 1.3 %copy-start.2 = (bf16[1,1,256,1,1,256]{5,2,4,3,1,0:T(8,128)(2,1)S(1)}, bf16[1,1,256,1,1,256]{5,2,4,3,1,0:T(8,128)(2,1)}, u32[]{:S(2)}) copy-start(bf16[1,1,256,1,1,256]{5,2,4,3,1,0:T(8,128)(2,1)} %param.11) | copy-start | bytes 393220
  2.0 1.3 %copy-start.3 = (bf16[1,1,256,256]{3,2,1,0:T(8,128)(2,1)S(1)}, bf16[1,1,256,256]{3,2,1,0:T(8,128)(2,1)}, u32[]{:S(2)}) copy-start(bf16[1,1,256,256]{3,2,1,0:T(8,128)(2,1)} %param.12) | copy-start | bytes 393220
  3.2 0.7 copy-start.4

commit v5 on v4

--- a/solution.py
+++ b/solution.py
@@ -70,25 +70,28 @@
     down = y * NZ + lax.rem(z + NZ - 1, NZ)
     half = B // 2
 
-    def f_copies(step, k):
-        up_slot = lax.rem(z + NZ - step, NZ)
-        down_slot = lax.rem(z + step, NZ)
-        if step < 3:
-            u, d = f_all.at[k, up_slot], f_all.at[k, down_slot]
+    def f_copies(stream, step):
+        k = min(stream, 2)
+        top, bottom = pl.ds(0, half), pl.ds(half, half)
+        if stream < 2:
+            ups, downs = (pl.ds(0, B), pl.ds(0, B)) if step < 3 else (top, bottom)
         else:
-            u = f_all.at[k, up_slot, pl.ds(0, half)]
-            d = f_all.at[k, down_slot, pl.ds(half, half)]
-        return (
-            remote(u, u, fs.at[0, step, k], fr.at[0, step, k], up, col),
-            remote(d, d, fs.at[1, step, k], fr.at[1, step, k], down, col),
-        )
-
-    def f_step(k, step):
+            ups = downs = top if stream == 2 else bottom
+        u = f_all.at[k, lax.rem(z + NZ - step, NZ), ups]
+        d = f_all.at[k, lax.rem(z + step, NZ), downs]
+        copies = []
+        if step < 3 or stream != 3:
+            copies.append(remote(u, u, fs.at[0, step, stream], fr.at[0, step, stream], up, col))
+        if step < 3 or stream != 2:
+            copies.append(remote(d, d, fs.at[1, step, stream], fr.at[1, step, stream], down, col))
+        return copies
+
+    def f_step(stream, step):
         if step > 0:
-            for copy in f_copies(step - 1, k):
+            for copy in f_copies(stream, step - 1):
                 copy.wait_recv()
         if step < 4:
-            for copy in f_copies(step, k):
+            for copy in f_copies(stream, step):
                 copy.start()
 
     slot = lax.rem(col, NZ)
@@ -244,46 +247,51 @@
     f_step(1, 0)
     near_own(0)
     f_step(0, 1)
+    f_step(1, 1)
     near_other(0)
-    f_step(1, 1)
+    f_step(0, 2)
     near_own(2)
+    f_step(1, 2)
+    f_step(2, 0)
     far_both(0)
-    f_step(0, 2)
     near_own(1)
     near_other(2)
-    f_step(1, 2)
+    f_step(0, 3)
+    f_step(3, 0)
+    f_step(1, 3)
+    f_step(2, 1)
     near_own(3)
     far_both(2)
     near_other(1)
-    f_step(0, 3)
-    f_step(2, 0)
-    f_step(1, 3)
+    f_step(3, 1)
+    f_step(0, 4)
+    f_step(2, 2)
     near_other(3)
     far_both(1)
     whole(2)
-    f_step(2, 1)
-    f_step(0, 4)
     send_early(0)
     f_step(1, 4)
     send_early(1)
+    f_step(3, 2)
+    f_step(2, 3)
     far_both(3)
     whole(1)
-    f_step(2, 2)
     send_up(0)
     send_up(1)
     whole(3)
     send_down(0)
     send_down(1)
-    f_step(2, 3)
+    f_step(3, 3)
     send_grown(0)
     send_grown(1)
+    f_step(2, 4)
+    f_step(3, 4)
+    send_early(2)
+    send_up(2)
+    send_down(2)
     whole(0)
     own(0)
     own(1)
-    f_step(2, 4)
-    send_early(2)
-    send_up(2)
-    send_down(2)
     own(2)
 
     def over_z(stage, src, dst):
@@ -315,6 +323,10 @@
     def arrived(stage):
         for copy in stages[stage]():
             copy.wait_recv()
+
+    def sent(stage):
+        for copy in stages[stage]():
+            copy.wait_send()
 
     def added(ref):
         return jnp.sum(ref[...].astype(f32), axis=0).astype(bf)
@@ -342,6 +354,33 @@
     arrived(0)
     s0_mid[y] = added(s0_in)
     start(2)
+    for stream in range(4):
+        for step in range(4):
+            for copy in f_copies(stream, step):
+                copy.wait_send()
+    for k in range(3):
+        for copies in (early(k), plain(k), grown(k)):
+            for copy in copies:
+                copy.wait_send()
+    for h in range(2):
+
+        @pl.when(2 * h + x // 2 != y)
+        def _():
+            a1_copy(h).wait_send()
+
+    @pl.when(hold == 1)
+    def _():
+        for k in range(NY):
+            y_copy(k, yl).wait_send()
+            for other in range(2):
+                o_copy(other, k).wait_send()
+
+    for k in range(NY):
+        for other in range(2):
+            x_copy(other, k).wait_send()
+            for far in range(2):
+                c_copy(far, other, k, core).wait_send()
+
     arrived(1)
     s1_mid[y] = added(s1_in)
     start(3)
@@ -351,6 +390,8 @@
     arrived(3)
     s1_out[z] = added(s1_mid)
     start(5)
+    for stage in range(4):
+        sent(stage)
     arrived(4)
     sums = s0_out[...].reshape(3, B, B).astype(f32)
     diag_a = d1_ref[0] - sums[0]
@@ -361,37 +402,11 @@
     pinv = (-(mm(parent_diag, pb) + sums[2])).astype(bf)
     pinv_ref[...] = pinv
     ahead = d2_ref[...] - mm_t(pb, pinv)
+    sent(4)
     arrived(5)
     diag2_ref[...] = ahead - s1_out[...].reshape(B, B).astype(f32)
 
-    for k in range(3):
-        for step in range(4):
-            for copy in f_copies(step, k):
-                copy.wait_send()
-        for copies in (early(k), plain(k), grown(k)):
-            for copy in copies:
-                copy.wait_send()
-    for h in range(2):
-
-        @pl.when(2 * h + x // 2 != y)
-        def _():
-            a1_copy(h).wait_send()
-
-    @pl.when(hold == 1)
-    def _():
-        for k in range(NY):
-            y_copy(k, yl).wait_send()
-            for other in range(2):
-                o_copy(other, k).wait_send()
-
-    for k in range(NY):
-        for other in range(2):
-            x_copy(other, k).wait_send()
-            for far in range(2):
-                c_copy(far, other, k, core).wait_send()
-    for stage in stages:
-        for copy in stage():
-            copy.wait_send()
+    sent(5)
 
 
 def body(anc, one, two, pb, d1, d2, p1, p2, par):
@@ -425,7 +440,7 @@
             pltpu.VMEM((NY, SLICE, B), bf), pltpu.VMEM((NZ, SLICE, B), bf),
         ]
         + [
-            dma((2, 4, 3)), dma((2, 4, 3)),
+            dma((2, 4, 4)), dma((2, 4, 4)),
             dma((2,)), dma((NY,)),
             dma((2, NY)), dma((2, NY)),
             dma((2, NY)), dma((2, NY)),

time: 109 us -> 107 us (0.982)
  the two profiles are of different devices: /device:TPU:8 before, /device:TPU:22 now
where the time goes in v5:
time: 107 us
  Pallas kernels  99.5 us (93%)
  local copies, waits for them, and re-layouts  5.64 us (5%)
  between operations  1.99 us (2%)
    pallas_call x1, Pallas kernels, body(): pl.pallas_call(kernel, out_shape=(jax.ShapeDtypeStruct((2, B, B), bf), ja...  99.5 us
    unnamed x15, local copies, waits for them, and re-layouts  4.45 us

profile of v5, /device:TPU:22, one launch (start us, length us, event | category | flops | bytes accessed | tf_op | source)
XLA Modules:
  0.0 107.1 jit_solution(17285955170609489320)
XLA Ops:
  1.9 0.0 copy-start
  1.9 0.0 copy-start.1
  1.9 0.0 copy-start.2
  2.0 0.0 copy-start.3
  2.0 1.2 %copy_bitcast_fusion = (bf16[2,256,256]{2,1,0:T(8,128)(2,1)S(1)}, bf16[2,256,256]{2,1,0:T(8,128)(2,1)S(1)}) fusion(bf16[1,1,256,2,1,256]{5,3,4,2,1,0:T(2,128)(2,1)} %param.10, bf16[1,1,256,2,1,256]{5,3,4,2,1,0:T(2,128)(2,1)} %param.9), kind=kLoop, calls=%fused_computation | loop fusion | bytes 1048576 | tf_op jit(solution)/shard_map/transpose | solution.py:414
  3.2 0.0 copy-start.4
  3.2 0.0 copy-done
  3.2 0.0 copy-done.1
  3.2 0.0 copy-done.2
  3.2 0.0 copy-done.3
  3.3 0.6 copy-done.4
  3.8 99.5 %shard_map.128 = (bf16[2,256,256]{2,1,0:T(8,128)(2,1)S(1)}, f32[2,256,256]{2,1,0:T(8,128)S(1)}, bf16[256,256]{1,0:T(8,128)(2,1)S(1)}, bf16[256,256]{1,0:T(8,128)(2,1)S(1)}, f32[256,256]{1,0:T(8,128)S(1)}) custom-call(s32[2]{0:T(128)S(1)} %bitcast.35, s32[1]{0:T(128)} %bitcast.24.p2_ref, s32[1]{0:T(128)} %bitcast.25.par_ref, ...), custom_call_target="tpu_custom_call" | custom-call | tf_op jit(solution)/shard_map/pallas_call | solution.py:419
  103.4 1.0 copy.16
  104.3 0.8 copy.26
  105.1 0.7 copy.27
  105.8 0.7 copy.28
  106.4 0.7 copy.29
Async XLA Ops:
  1.9 1.2 %copy-start = (f32[2,1,256,256]{3,2,1,0:T(8,128)S(1)}, f32[2,1,256,256]{3,2,1,0:T(8,128)}, u32[]{:S(2)}) copy-start(f32[2,1,256,256]{3,2,1,0:T(8,128)} %param.13) | copy-start | bytes 1572868
  1.9 1.3 %copy-start.1 = (f32[1,1,256,256]{3,2,1,0:T(8,128)S(1)}, f32[1,1,256,256]{3,2,1,0:T(8,128)}, u32[]{:S(2)}) copy-start(f32[1,1,256,256]{3,2,1,0:T(8,128)} %param.14) | copy-start | bytes 786436
  1.9 1.3 %copy-start.2 = (bf16[1,1,256,1,1,256]{5,2,4,3,1,0:T(8,128)(2,1)S(1)}, bf16[1,1,256,1,1,256]{5,2,4,3,1,0:T(8,128)(2,1)}, u32[]{:S(2)}) copy-start(bf16[1,1,256,1,1,256]{5,2,4,3,1,0:T(8,128)(2,1)} %param.11) | copy-start | bytes 393220
  2.0 1.3 %copy-start.3 = (bf16[1,1,256,256]{3,2,1,0:T(8,128)(2,1)S(1)}, bf16[1,1,256,256]{3,2,1,0:T(8,128)(2,1)}, u32[]{:S(2)}) copy-start(bf16[1,1,256,256]{3,2,1,0:T(8,128)(2,1)} %param.12) | copy-start | bytes 393220
  3.2 0.7 copy-start.4

commit v6 on v5

--- a/solution.py
+++ b/solution.py
@@ -296,7 +296,8 @@
 
     def over_z(stage, src, dst):
         return [
-            remote(src(d), dst(d), ss.at[stage, d], sr.at[stage, d], z_mate(d), col) for d in range(1, NZ)
+            remote(src(d), dst(d), ss.at[stage, d], sr.at[stage, d], z_mate(d), col)
+            for d in (4, 3, 5, 2, 6, 1, 7)
         ]
 
     def over_y(stage, src, dst):

time: 107 us -> 106 us (level)
  the two profiles are of different devices: /device:TPU:22 before, /device:TPU:2 now
where the time goes in v6:
time: 106 us
  Pallas kernels  98.6 us (93%)
  local copies, waits for them, and re-layouts  5.64 us (5%)
  between operations  1.99 us (2%)
    pallas_call x1, Pallas kernels, body(): pl.pallas_call(kernel, out_shape=(jax.ShapeDtypeStruct((2, B, B), bf), ja...  98.6 us
    unnamed x15, local copies, waits for them, and re-layouts  4.45 us

profile of v6, /device:TPU:2, one launch (start us, length us, event | category | flops | bytes accessed | tf_op | source)
XLA Modules:
  0.0 106.2 jit_solution(2354670691755161500)
XLA Ops:
  1.9 0.0 copy-start
  1.9 0.0 copy-start.1
  1.9 0.0 copy-start.2
  2.0 0.0 copy-start.3
  2.0 1.2 %copy_bitcast_fusion = (bf16[2,256,256]{2,1,0:T(8,128)(2,1)S(1)}, bf16[2,256,256]{2,1,0:T(8,128)(2,1)S(1)}) fusion(bf16[1,1,256,2,1,256]{5,3,4,2,1,0:T(2,128)(2,1)} %param.10, bf16[1,1,256,2,1,256]{5,3,4,2,1,0:T(2,128)(2,1)} %param.9), kind=kLoop, calls=%fused_computation | loop fusion | bytes 1048576 | tf_op jit(solution)/shard_map/transpose | solution.py:415
  3.2 0.0 copy-start.4
  3.2 0.0 copy-done
  3.2 0.0 copy-done.1
  3.2 0.0 copy-done.2
  3.2 0.0 copy-done.3
  3.3 0.6 copy-done.4
  3.8 98.6 %shard_map.128 = (bf16[2,256,256]{2,1,0:T(8,128)(2,1)S(1)}, f32[2,256,256]{2,1,0:T(8,128)S(1)}, bf16[256,256]{1,0:T(8,128)(2,1)S(1)}, bf16[256,256]{1,0:T(8,128)(2,1)S(1)}, f32[256,256]{1,0:T(8,128)S(1)}) custom-call(s32[2]{0:T(128)S(1)} %bitcast.35, s32[1]{0:T(128)} %bitcast.24.p2_ref, s32[1]{0:T(128)} %bitcast.25.par_ref, ...), custom_call_target="tpu_custom_call" | custom-call | tf_op jit(solution)/shard_map/pallas_call | solution.py:420
  102.4 1.0 copy.16
  103.4 0.8 copy.26
  104.2 0.7 copy.27
  104.9 0.7 copy.28
  105.5 0.7 copy.29
Async XLA Ops:
  1.9 1.2 %copy-start = (f32[2,1,256,256]{3,2,1,0:T(8,128)S(1)}, f32[2,1,256,256]{3,2,1,0:T(8,128)}, u32[]{:S(2)}) copy-start(f32[2,1,256,256]{3,2,1,0:T(8,128)} %param.13) | copy-start | bytes 1572868
  1.9 1.3 %copy-start.1 = (f32[1,1,256,256]{3,2,1,0:T(8,128)S(1)}, f32[1,1,256,256]{3,2,1,0:T(8,128)}, u32[]{:S(2)}) copy-start(f32[1,1,256,256]{3,2,1,0:T(8,128)} %param.14) | copy-start | bytes 786436
  1.9 1.3 %copy-start.2 = (bf16[1,1,256,1,1,256]{5,2,4,3,1,0:T(8,128)(2,1)S(1)}, bf16[1,1,256,1,1,256]{5,2,4,3,1,0:T(8,128)(2,1)}, u32[]{:S(2)}) copy-start(bf16[1,1,256,1,1,256]{5,2,4,3,1,0:T(8,128)(2,1)} %param.11) | copy-start | bytes 393220
  2.0 1.3 %copy-start.3 = (bf16[1,1,256,256]{3,2,1,0:T(8,128)(2,1)S(1)}, bf16[1,1,256,256]{3,2,1,0:T(8,128)(2,1)}, u32[]{:S(2)}) copy-start(bf16[1,1,256,256]{3,2,1,0:T(8,128)(2,1)} %param.12) | copy-start | bytes 393220
  3.2 0.7 copy-start.4
